TPU v7x, 32 devices: a whole 2x2x4 slice. The times are simulated.
32 devices in a mesh: groups: 2 (over x), tile: 16 (over z, y, core).
Axes of the slice: x: 2, y: 2, z: 4, core: 2. Of those that a mesh axis runs over, the one named last changes fastest.
Arguments:
- image: float32 [4, 768, 4096], P(None, ('groups', 'tile')), parts along dimension 1, may hold values from -6 to 6
- inv_var: float32 [4, 768, 4096], P(None, ('groups', 'tile')), parts along dimension 1, may hold values from 0.25 to 4
- shift: float32 [8, 2], P('groups'), parts along dimension 0, may hold values from -0.5 to 0.5
- col_offset: int32 [8], P('groups'), parts along dimension 0, may hold values from -8 to 8
- psf_rows: float32 [8, 3, 41], P('groups'), parts along dimension 0, may hold values from -1 to 1
- psf_cols: float32 [8, 3, 41], P('groups'), parts along dimension 0, may hold values from -0.5 to 0.5
- placement: int32 [4096, 1], P(('groups', 'tile')), parts along dimension 0, may hold values from 0 to 15; in each aligned block of 128 rows (0 to 127, 128 to 255, ...) at most 16 rows name the same one
Outputs:
- matched: bfloat16 [4, 768, 4096], P(None, ('groups', 'tile')), parts along dimension 1
- coadd: float32 [32, 24, 128], P(('groups', 'tile')), parts along dimension 0
There are 2 independent parts, one for each index of `groups`. A program takes and returns all parts, laid end to end along the dimension named above; each array names one. Nothing has to cross between parts.
Inputs may be any that keep to these rules, and one draw needn't show every extreme that they name: `placement`: every patch receives at least one piece; within the pieces of one device no patch is named more than 16 times, a bound that some block reaches.
All inputs are finite; a program needn't handle non-finite values.
Results may differ from a plain program's by a relative error of at most 0.001.
Values sent between devices are 32-bit elements; how exact they have to be, the bound alone decides.
No kernel may reach another device: no remote copies, remote signals or barrier semaphores. Data moves between devices by JAX's collectives and lax.ppermute only.
A program may use at most 192 MiB of HBM per device.

v0:
```python
import jax
import jax.numpy as jnp
from jax import lax
from jax.sharding import PartitionSpec as P

PC = 128


def padded_2(x, sides, width):
    for axis, dim in sides:
        size, length = (lax.axis_size(axis), x.shape[dim])
        up = [(i, (i + 1) % size) for i in range(size - 1)]
        down = [(j, i) for i, j in up]
        last = lax.slice_in_dim(x, length - width, length, axis=dim)
        leading = lax.slice_in_dim(x, 0, width, axis=dim)
        before = lax.ppermute(last, axis, up)
        after = lax.ppermute(leading, axis, down)
        x = jnp.concatenate([before, x, after], axis=dim)
    return x


def lanczos(values):
    return jnp.where(jnp.abs(values) < 3.0, jnp.sinc(values) * jnp.sinc(values / 3.0), 0.0)


def tap_weights(fraction):
    places = jnp.arange(-3, 4).astype(jnp.float32)
    weights = lanczos(places[None, :] + fraction[:, None])
    return weights / jnp.sum(weights, axis=1, keepdims=True)


def warp(extended, shift, col_offset):
    height = extended.shape[1] - 6
    width = extended.shape[2]
    row_weight = tap_weights(shift[:, 0])
    col_weight = tap_weights(shift[:, 1])
    shifted = jnp.zeros((extended.shape[0], height, width), jnp.float32)
    for place in range(-3, 4):
        shifted = (
            shifted
            + row_weight[:, place + 3, None, None] * extended[:, 3 - place : 3 - place + height]
        )
    padded = jnp.pad(shifted, ((0, 0), (0, 0), (11, 11)))

    def one_visit(plane, weights, offset):
        total = jnp.zeros((height, width), jnp.float32)
        for place in range(-3, 4):
            start = 11 - offset - place
            total = total + weights[place + 3] * lax.dynamic_slice_in_dim(plane, start, width, 1)
        return total

    return jax.vmap(one_visit)(padded, col_weight, col_offset)


def band_table(kernel, count):
    outer = jnp.arange(count, dtype=jnp.int32)[:, None]
    inner = jnp.arange(count + 40, dtype=jnp.int32)[None, :]
    index = outer + 40 - inner
    select = (index[:, :, None] == jnp.arange(41, dtype=jnp.int32)[None, None, :]).astype(
        jnp.float32
    )
    return jnp.einsum("vkt,oit->vkoi", kernel, select, precision=lax.Precision.HIGHEST)


def on_device(image, inv_var, shift, col_offset, psf_rows, psf_cols, placement):
    visits, height, width = image.shape
    raw = padded_2(image, (("tile", 1),), 3)
    warped = warp(raw, shift, col_offset)
    extended = padded_2(warped, (("tile", 1),), 20)
    row_band = band_table(psf_rows, height)
    along = jnp.einsum("vkim,vmw->vkiw", row_band, extended, precision=lax.Precision.HIGHEST)
    padded = jnp.pad(along, ((0, 0), (0, 0), (0, 0), (20, 20)))
    blocks = width // 128
    windows = jnp.stack(
        [padded[..., block * 128 : block * 128 + 168] for block in range(blocks)], axis=3
    )
    col_band = band_table(psf_cols, 128)
    matched = jnp.einsum("vkinw,vkow->vino", windows, col_band, precision=lax.Precision.HIGHEST)
    matched = matched.reshape(visits, height, width)
    pieces = width // PC
    labels = placement.reshape(visits, pieces)
    stacked = jnp.stack((inv_var * matched, inv_var)).reshape(2, visits, height, pieces, PC)
    owners = jnp.arange(1 * lax.axis_size("tile"), dtype=jnp.int32)
    onehot = (labels[None] == owners[:, None, None]).astype(jnp.float32)
    sums = lax.psum_scatter(
        jnp.einsum("pvc,svrcx->psrx", onehot, stacked, precision=lax.Precision.HIGHEST),
        "tile",
        scatter_dimension=0,
        tiled=True,
    )
    coadd = sums[:, 0] / jnp.maximum(sums[:, 1], 1.0)
    return (matched.astype(jnp.bfloat16), coadd)


def solution(mesh):
    in_specs = (
        P(None, ("groups", "tile"), None),
        P(None, ("groups", "tile"), None),
        P("groups", None),
        P("groups"),
        P("groups", None, None),
        P("groups", None, None),
        P(("groups", "tile"), None),
    )
    out_specs = (P(None, ("groups", "tile"), None), P(("groups", "tile"), None, None))
    return jax.shard_map(
        on_device, mesh=mesh, in_specs=in_specs, out_specs=out_specs, check_vma=False
    )
```

profile of v0, /device:TPU:0, one launch (start us, length us, event | category | flops | bytes accessed | tf_op | source)
XLA Modules:
  0.0 230.0 jit_solution(13277037182643720478)
XLA Ops:
  9.8 3.0 %collective-permute-start.1 = (f32[4,3,4096]{2,1,0:T(4,128)S(1)}, f32[4,3,4096]{2,1,0:T(4,128)S(1)}, u32[]{:S(2)}, u32[]{:S(2)}) collective-permute-start(f32[4,3,4096]{2,1,0:T(4,128)S(1)} %get-tuple-element.246), channel_id=1, source_target_pairs={{0,1},{1,2},{2,3},{3,4},{4,5},{5,6},{6,7},{7,8},{8,9},{9,10},{10,1... | collective-permute-start | bytes 589832 | tf_op jit(solution)/shard_map/ppermute | solution.py:16
  12.9 1.5 constant_dynamic-update-slice_fusion.1
  15.5 4.6 %fusion.15 = f32[4,24,4096]{2,1,0:T(8,128)S(1)} fusion(f32[4,24,4096]{2,1,0:T(8,128)} %param.8, f32[4,3,4096]{2,1,0:T(4,128)S(1)} %collective-permute-done.1, f32[4,27,4096]{2,1,0:T(8,128)S(1)} %constant_dynamic-update-slice_fusion, f32[4]{0:T(128)S(1)} %get-tuple-element.255, f32[4]{0:T(128)S(1)} %get-tuple-element.256, f32[4]{0:T(128)S(1)} %get-tuple-element.257, ...), kind=kLoop, calls=%fused_computation.37 | loop fusion | flops 6291456 | bytes 8061040 | tf_op jit(solution)/shard_map/add | solution.py:40
  20.8 8.1 %while.7 = (s32[]{:T(128)}, f32[4,24,4118]{2,1,0:T(8,128)S(1)}, s32[4,3]{1,0:T(4,128)S(1)}, f32[4,24,4096]{2,1,0:T(8,128)S(1)}, s32[]{:T(128)}) while((s32[]{:T(128)}, f32[4,24,4118]{2,1,0:T(8,128)S(1)}, s32[4,3]{1,0:T(4,128)S(1)}, f32[4,24,4096]{2,1,0:T(8,128)S(1)}, s32[]{:T(128)}) %tuple.183), condition=%wide.while_cond, body=%wide.while_body.sunk | while | flops 2 | bytes 786549 | solution.py:49
  28.9 1.4 broadcast.155.clone.5
  30.6 10.8 %while.8 = (s32[]{:T(128)}, f32[4,24,4118]{2,1,0:T(8,128)S(1)}, s32[4,3]{1,0:T(4,128)S(1)}, f32[4,24,4096]{2,1,0:T(8,128)}, s32[]{:T(128)}) while((s32[]{:T(128)}, f32[4,24,4118]{2,1,0:T(8,128)S(1)}, s32[4,3]{1,0:T(4,128)S(1)}, f32[4,24,4096]{2,1,0:T(8,128)}, s32[]{:T(128)}) %tuple.188), condition=%wide.while_cond.1, body=%wide.while_body.1.sunk | while | flops 2 | bytes 788073 | solution.py:49
  31.1 2.1 dynamic-slice_dynamic-update-slice_fusion.15
  33.8 2.1 dynamic-slice_dynamic-update-slice_fusion.15
  36.5 2.1 dynamic-slice_dynamic-update-slice_fusion.15
  39.2 2.1 dynamic-slice_dynamic-update-slice_fusion.15
  41.4 8.5 %while.9 = (s32[]{:T(128)}, f32[4,24,4118]{2,1,0:T(8,128)S(1)}, s32[4,3]{1,0:T(4,128)S(1)}, f32[4,24,4096]{2,1,0:T(8,128)S(1)}, s32[]{:T(128)}) while((s32[]{:T(128)}, f32[4,24,4118]{2,1,0:T(8,128)S(1)}, s32[4,3]{1,0:T(4,128)S(1)}, f32[4,24,4096]{2,1,0:T(8,128)S(1)}, s32[]{:T(128)}) %tuple.189), condition=%wide.while_cond.2, body=%wide.while_body.2.sunk | while | flops 2 | bytes 786549 | solution.py:49
  42.1 1.4 dynamic-slice_dynamic-update-slice_fusion.16
  44.2 1.4 dynamic-slice_dynamic-update-slice_fusion.16
  48.5 1.4 dynamic-slice_dynamic-update-slice_fusion.16
  49.9 1.5 broadcast.155.clone.3
  51.7 11.4 %while.10 = (s32[]{:T(128)}, f32[4,24,4118]{2,1,0:T(8,128)S(1)}, s32[4,3]{1,0:T(4,128)S(1)}, f32[4,24,4096]{2,1,0:T(8,128)}, s32[]{:T(128)}) while((s32[]{:T(128)}, f32[4,24,4118]{2,1,0:T(8,128)S(1)}, s32[4,3]{1,0:T(4,128)S(1)}, f32[4,24,4096]{2,1,0:T(8,128)}, s32[]{:T(128)}) %tuple.190), condition=%wide.while_cond.3, body=%wide.while_body.3.sunk | while | flops 2 | bytes 788073 | solution.py:49
  52.3 2.2 dynamic-slice_dynamic-update-slice_fusion.17
  55.2 2.2 dynamic-slice_dynamic-update-slice_fusion.17
  58.1 2.2 dynamic-slice_dynamic-update-slice_fusion.17
  60.9 2.2 dynamic-slice_dynamic-update-slice_fusion.17
  63.2 8.2 %while.11 = (s32[]{:T(128)}, f32[4,24,4118]{2,1,0:T(8,128)S(1)}, s32[4,3]{1,0:T(4,128)S(1)}, f32[4,24,4096]{2,1,0:T(8,128)S(1)}, s32[]{:T(128)}) while((s32[]{:T(128)}, f32[4,24,4118]{2,1,0:T(8,128)S(1)}, s32[4,3]{1,0:T(4,128)S(1)}, f32[4,24,4096]{2,1,0:T(8,128)S(1)}, s32[]{:T(128)}) %tuple.191), condition=%wide.while_cond.4, body=%wide.while_body.4.sunk | while | flops 2 | bytes 786549 | solution.py:49
  63.8 1.4 dynamic-slice_dynamic-update-slice_fusion.18
  65.9 1.4 dynamic-slice_dynamic-update-slice_fusion.18
  68.0 1.4 dynamic-slice_dynamic-update-slice_fusion.18
  70.0 1.4 dynamic-slice_dynamic-update-slice_fusion.18
  71.5 1.4 broadcast.155.clone.1
  73.2 11.4 %while.12 = (s32[]{:T(128)}, f32[4,24,4118]{2,1,0:T(8,128)S(1)}, s32[4,3]{1,0:T(4,128)S(1)}, f32[4,24,4096]{2,1,0:T(8,128)}, s32[]{:T(128)}) while((s32[]{:T(128)}, f32[4,24,4118]{2,1,0:T(8,128)S(1)}, s32[4,3]{1,0:T(4,128)S(1)}, f32[4,24,4096]{2,1,0:T(8,128)}, s32[]{:T(128)}) %tuple.192), condition=%wide.while_cond.5, body=%wide.while_body.5.sunk | while | flops 2 | bytes 788073 | solution.py:49
  73.8 2.2 dynamic-slice_dynamic-update-slice_fusion.19
  76.7 2.2 dynamic-slice_dynamic-update-slice_fusion.19
  79.5 2.2 dynamic-slice_dynamic-update-slice_fusion.19
  82.4 2.2 dynamic-slice_dynamic-update-slice_fusion.19
  84.7 8.3 %while.13 = (s32[]{:T(128)}, f32[4,24,4118]{2,1,0:T(8,128)S(1)}, s32[4,3]{1,0:T(4,128)S(1)}, f32[4,24,4096]{2,1,0:T(8,128)S(1)}, s32[]{:T(128)}) while((s32[]{:T(128)}, f32[4,24,4118]{2,1,0:T(8,128)S(1)}, s32[4,3]{1,0:T(4,128)S(1)}, f32[4,24,4096]{2,1,0:T(8,128)S(1)}, s32[]{:T(128)}) %tuple.193), condition=%wide.while_cond.6, body=%wide.while_body.6.sunk | while | flops 2 | bytes 786549 | solution.py:49
  85.3 1.5 dynamic-slice_dynamic-update-slice_fusion.20
  87.4 1.5 dynamic-slice_dynamic-update-slice_fusion.20
  89.5 1.5 dynamic-slice_dynamic-update-slice_fusion.20
  91.6 1.5 dynamic-slice_dynamic-update-slice_fusion.20
  94.2 5.4 %multiply_add_fusion = f32[4,24,4096]{2,1,0:T(8,128)S(1)} fusion(f32[4,24,4096]{2,1,0:T(8,128)} %copy-done.2, f32[4,24,4096]{2,1,0:T(8,128)} %get-tuple-element.50, f32[4,24,4096]{2,1,0:T(8,128)} %copy-done.5, f32[4,24,4096]{2,1,0:T(8,128)} %get-tuple-element.34, f32[4,24,4096]{2,1,0:T(8,128)} %copy-done.4, f32[4,24,4096]{2,1,0:T(8,128)} %get-tuple-element.18, ...), kind=kLoop, calls=%fused_computation.52 | loop fusion | flops 5111808 | bytes 12583024 | tf_op jit(solution)/shard_map/vmap()/add | solution.py:49
  99.9 1.9 copy.59
  101.8 8.1 %collective-permute-start.2 = (f32[4,20,4096]{2,0,1:T(4,128)}, f32[4,20,4096]{2,0,1:T(4,128)}, u32[]{:S(2)}, u32[]{:S(2)}) collective-permute-start(f32[4,20,4096]{2,0,1:T(4,128)} %copy.59), channel_id=1, source_target_pairs={{0,1},{1,2},{2,3},{3,4},{4,5},{5,6},{6,7},{7,8},{8,9},{9,10},{10,1... | collective-permute-start | bytes 3932168 | tf_op jit(solution)/shard_map/ppermute | solution.py:16
  109.9 1.9 copy.60
  113.6 4.8 %copy.73 = pred[128,168,41,1]{1,2,3,0:T(8,128)(4,1)} copy(pred[128,168,41,1]{0,1,2,3:T(8,128)(4,1)S(1)} %fusion.7) | data formatting | bytes 1763328 | tf_op jit(solution)/shard_map/eq | solution.py:59
  118.4 1.7 copy.87
  121.4 3.6 %convolution_bitcast_fusion = f32[4,3,128,168,1]{3,0,1,2,4:T(4,128)S(1)} fusion(pred[128,168,41,1]{1,2,3,0:T(8,128)(4,1)} %copy.73, f32[4,3,41]{2,0,1:T(4,128)S(1)} %copy-done), kind=kOutput, calls=%fused_computation.54 | convolution fusion | flops 126959616 | bytes 1915824 | tf_op jit(solution)/shard_map/vkt,oit->vkoi/dot_general | solution.py:62
  125.4 2.1 copy.61
  127.5 2.1 copy.62
  129.6 4.3 %fusion.2 = f32[4,3,24,4096]{3,2,1,0:T(8,128)S(1)} fusion(f32[4,20,4096]{2,1,0:T(8,128)S(1)} %copy.62, f32[4,24,4096]{2,1,0:T(8,128)S(1)} %multiply_add_fusion, f32[4,20,4096]{2,1,0:T(8,128)S(1)} %copy.61, f32[4,3,24,64]{3,0,1,2:T(4,128)S(1)} %convolution_bitcast_fusion.1), kind=kOutput, calls=%fused_computation.19 | convolution fusion | flops 908066816 | bytes 8986624 | tf_op jit(solution)/shard_map/vkim,vmw->vkiw/dot_general | solution.py:71
  138.6 8.6 %fusion.24 = f32[4,32,3,8,128]{4,3,2,1,0:T(8,128)S(1)} fusion(f32[4,3,128,168,1]{3,0,1,2,4:T(4,128)S(1)} %convolution_bitcast_fusion, f32[4,3,24,32,168]{4,2,1,0,3:T(8,128)S(1)} %fusion.37), kind=kOutput, calls=%fused_computation.53 | convolution fusion | flops 2378170368 | bytes 8798208 | tf_op jit(solution)/shard_map/vkinw,vkow->vino/dot_general | solution.py:78
  150.9 71.0 %reduce-scatter.2.cloned.1.call-done = f32[1,2,24,128]{3,2,1,0:T(8,128)} async-done(((f32[16,2,24,128]{3,2,1,0:T(8,128)}), f32[1,2,24,128]{3,2,1,0:T(8,128)}) %reduce-scatter.2.cloned.1.call-update) | async-done | bytes 24592 | tf_op jit(solution)/shard_map/reduce_scatter | solution.py:85
  (160 shorter events, 44.1 us)
Async XLA Ops:
  7.2 114.3 %copy-start = (f32[4,3,41]{2,0,1:T(4,128)S(1)}, f32[4,3,41]{2,0,1:T(4,128)}, u32[]{:S(2)}) copy-start(f32[4,3,41]{2,0,1:T(4,128)} %param.13) | copy-start | bytes 5908
  7.2 214.7 %reduce-scatter.2.cloned.1.call-start = ((), (), s32[]{:S(2)}) async-start(), calls=%async_computation.1 | async-start | bytes 417792 | tf_op jit(solution)/shard_map/reduce_scatter | solution.py:85
  8.5 5.9 %copy-start.7 = (f32[4,2]{0,1:T(2,128)S(1)}, f32[4,2]{0,1:T(2,128)}, u32[]{:S(2)}) copy-start(f32[4,2]{0,1:T(2,128)} %param.10) | copy-start | bytes 100
  8.5 6.1 %copy-start.8 = (s32[4]{0:T(128)S(1)}, s32[4]{0:T(128)}, u32[]{:S(2)}) copy-start(s32[4]{0:T(128)} %param.11) | copy-start | bytes 52
  8.5 6.8 %collective-permute-start = (f32[4,3,4096]{2,1,0:T(4,128)S(1)}, f32[4,3,4096]{2,1,0:T(4,128)S(1)}, u32[]{:S(2)}, u32[]{:S(2)}) collective-permute-start(f32[4,3,4096]{2,1,0:T(4,128)S(1)} %get-tuple-element.245), channel_id=1, source_target_pairs={{1,0},{2,1},{3,2},{4,3},{5,4},{6,5},{7,6},{8,7},{9,8},{10,9},{11,1... | collective-permute-start | bytes 589832 | tf_op jit(solution)/shard_map/ppermute | solution.py:17
  9.8 5.6 %collective-permute-start.1 = (f32[4,3,4096]{2,1,0:T(4,128)S(1)}, f32[4,3,4096]{2,1,0:T(4,128)S(1)}, u32[]{:S(2)}, u32[]{:S(2)}) collective-permute-start(f32[4,3,4096]{2,1,0:T(4,128)S(1)} %get-tuple-element.246), channel_id=1, source_target_pairs={{0,1},{1,2},{2,3},{3,4},{4,5},{5,6},{6,7},{7,8},{8,9},{9,10},{10,1... | collective-permute-start | bytes 589832 | tf_op jit(solution)/shard_map/ppermute | solution.py:16
  28.9 1.7 copy-start.3
  49.9 1.7 copy-start.4
  71.5 1.7 copy-start.5
  93.0 1.2 copy-start.2
  101.8 23.6 %collective-permute-start.2 = (f32[4,20,4096]{2,0,1:T(4,128)}, f32[4,20,4096]{2,0,1:T(4,128)}, u32[]{:S(2)}, u32[]{:S(2)}) collective-permute-start(f32[4,20,4096]{2,0,1:T(4,128)} %copy.59), channel_id=1, source_target_pairs={{0,1},{1,2},{2,3},{3,4},{4,5},{5,6},{6,7},{7,8},{8,9},{9,10},{10,1... | collective-permute-start | bytes 3932168 | tf_op jit(solution)/shard_map/ppermute | solution.py:16
  111.8 15.7 %collective-permute-start.3 = (f32[4,20,4096]{2,0,1:T(4,128)}, f32[4,20,4096]{2,0,1:T(4,128)}, u32[]{:S(2)}, u32[]{:S(2)}) collective-permute-start(f32[4,20,4096]{2,0,1:T(4,128)} %copy.60), channel_id=1, source_target_pairs={{1,0},{2,1},{3,2},{4,3},{5,4},{6,5},{7,6},{8,7},{9,8},{10,9},{11,1... | collective-permute-start | bytes 3932168 | tf_op jit(solution)/shard_map/ppermute | solution.py:17
  118.4 2.2 copy-start.9
  120.1 5.0 %copy-start.6 = (f32[4,3,41]{2,0,1:T(4,128)S(1)}, f32[4,3,41]{2,0,1:T(4,128)}, u32[]{:S(2)}) copy-start(f32[4,3,41]{2,0,1:T(4,128)} %param.12) | copy-start | bytes 5908
  138.6 8.7 %copy-start.1 = (f32[4,24,4096]{2,1,0:T(8,128)S(1)}, f32[4,24,4096]{2,1,0:T(8,128)}, u32[]{:S(2)}) copy-start(f32[4,24,4096]{2,1,0:T(8,128)} %param.9) | copy-start | bytes 4718596
Sparse Core Ops, SparseCore 0:
  149.9 71.8 reduce-scatter.1
where the time goes:
time: 231 us; the launch traced here: 230 us
  local copies, waits for them, and re-layouts  99 us (43%)
  waiting for transfers between devices  71 us (31%)
  matrix products  18.1 us (8%)
  between operations  14.7 us (6%)
  starting transfers between devices  13.7 us (6%)
  other arithmetic  13 us (6%)
    reduce_scatter x1, waiting for transfers between devices, on_device(): lax.psum_scatter(jnp.einsum('pvc,svrcx->psrx', onehot, stacked, precision...  71 us
    gather x84, local copies, waits for them, and re-layouts  66.2 us
    unnamed x70, local copies, waits for them, and re-layouts  15.8 us
    ppermute x2, starting transfers between devices, padded_2(): before = lax.ppermute(last, axis, up)  11.1 us
    dot_general x1, matrix products, on_device(): jnp.einsum('vkinw,vkow->vino', windows, col_band, precision=lax.Precision...  8.64 us
    add x1, other arithmetic, one_visit(): total + weights[place + 3] * lax.dynamic_slice_in_dim(plane, start, width...  5.38 us
    eq x1, local copies, waits for them, and re-layouts, band_table(): index[:, :, None] == jnp.arange(41, dtype=jnp.int32)[None, None, :]  4.76 us
    add x1, other arithmetic, warp(): shifted + row_weight[:, place + 3, None, None] * extended[:, 3 - place:3...  4.63 us
  transfers between devices with their start and end apart: 5, of which 1 were waited for; matrix products, arithmetic and copies ran while one was open for 9% of the time, Pallas kernels for 0%

commit v1 on v0

v1 whole, which is shorter than its diff:
```python
import functools
import jax
import jax.numpy as jnp
from jax import lax
from jax.experimental import pallas as pl
from jax.experimental.pallas import tpu as pltpu
from jax.sharding import PartitionSpec as P

PC = 128
F32 = jnp.float32
BF16 = jnp.bfloat16
HIGHEST = lax.Precision.HIGHEST


def lanczos(values):
    return jnp.where(jnp.abs(values) < 3.0, jnp.sinc(values) * jnp.sinc(values / 3.0), 0.0)


def tap_weights(fraction):
    places = jnp.arange(-3, 4).astype(jnp.float32)
    weights = lanczos(places[None, :] + fraction[:, None])
    return weights / jnp.sum(weights, axis=1, keepdims=True)


def round_up(number, unit):
    return -(-number // unit) * unit


def split(x):
    high = x.astype(BF16)
    low = (x - high.astype(F32)).astype(BF16)
    return high, low


def band(vector, rows, lanes, shift):
    wide = vector.shape[-1]
    turned = pltpu.roll(jnp.broadcast_to(vector, (8, wide)), shift, 1)[:1]
    full = jnp.broadcast_to(turned, (rows, wide))
    return pltpu.roll(full, 0, 1, stride=1, stride_axis=0)[:, :lanes]


def prepare_kernel(
    bases, length, height, slots_ref, scal_ref, vecs_ref, inv_ref, rows_ref, cols_ref, edge_ref, den_ref
):
    visit = pl.program_id(0)
    half = length // 2
    ext = 3 * height
    pad = round_up(ext, 16)
    base = vecs_ref[0]
    psf = [band(base[k : k + 1, :PC], height, PC, height + half - (length - 1)) for k in range(bases)]
    psf = jnp.concatenate(psf, axis=0)
    warp = band(base[2 * bases : 2 * bases + 1, :PC], PC, PC, PC - 3)
    place = lax.broadcasted_iota(jnp.int32, (PC, PC), 0) + scal_ref[0] - height
    warp = jnp.where((place >= 0) & (place < scal_ref[1]), warp, 0.0)
    rows = jnp.dot(psf, warp, precision=HIGHEST, preferred_element_type=F32)
    lane = lax.broadcasted_iota(jnp.int32, rows.shape, 1)
    rows = jnp.where(lane < ext, rows, 0.0)
    high = rows.astype(BF16).astype(F32)
    low = rows - high
    blank = jnp.zeros_like(rows)
    high = jnp.concatenate([high, blank], axis=1)
    low = jnp.concatenate([low, blank], axis=1)
    rows_ref[0] = (high + pltpu.roll(low, pad, 1) + pltpu.roll(high, 2 * pad, 1)).astype(BF16)
    wide = 2 * PC
    psf = [
        band(base[bases + k : bases + k + 1], wide, PC, wide - (PC // 2 + half))
        for k in range(bases)
    ]
    warp = band(base[2 * bases + 1 : 2 * bases + 2], wide, wide, lax.rem(scal_ref[2 + visit] + wide - 3, wide))
    left_c = lax.broadcasted_iota(jnp.int32, (wide, wide), 0) < PC
    left_m = lax.broadcasted_iota(jnp.int32, (wide, wide), 1) < PC
    warp_edge = jnp.where(left_c == left_m, warp, 0.0)
    left_r = lax.broadcasted_iota(jnp.int32, (wide, PC), 0) < PC
    left_q = lax.broadcasted_iota(jnp.int32, (wide, PC), 1) < PC // 2
    for k in range(bases):
        for out, first, second in (
            (cols_ref, warp, psf[k]),
            (edge_ref, warp_edge, jnp.where(left_r == left_q, psf[k], 0.0)),
        ):
            both = jnp.dot(first, second, precision=HIGHEST, preferred_element_type=F32)
            high, low = split(both)
            out[0, k * wide : (k + 1) * wide, :PC] = high
            out[0, k * wide : (k + 1) * wide, PC:] = low

    @pl.when(visit == 0)
    def _():
        den_ref[...] = jnp.zeros_like(den_ref)

    pieces = inv_ref.shape[2] // PC
    for c in range(pieces):
        slot = slots_ref[visit * pieces + c]
        den_ref[slot] += inv_ref[0, :, c * PC : (c + 1) * PC]


def match_kernel(
    bases, first, last, slots_ref, up_ref, own_ref, down_ref, inv_ref, rows_ref, cols_ref, edge_ref,
    out_ref, send_ref, keep_ref, high_ref, low_ref, acc_ref
):
    step = pl.program_id(0)
    visit = step + first
    height, width = own_ref.shape[1], own_ref.shape[2]
    pieces = width // PC
    pairs = pieces // 2
    pad = round_up(3 * height, 16)
    deep = rows_ref.shape[2]
    operator = rows_ref[0]

    def columns(ref, pair):
        return [ref[0, :, n * PC : (n + 1) * PC] for n in (pair, pair + pairs)]

    def store(pair, along, order):
        for k in range(bases):
            block = [along[k * height : (k + 1) * height, h * PC : (h + 1) * PC] for h in order]
            high, low = split(jnp.concatenate(block, axis=0))
            high_ref[k, pair * 2 * height : (pair + 1) * 2 * height, :] = high
            low_ref[k, pair * 2 * height : (pair + 1) * 2 * height, :] = low

    for pair in range(pairs):
        parts = [columns(ref, pair) for ref in (up_ref, own_ref, down_ref)]
        stacked = jnp.concatenate([jnp.concatenate(part, axis=1) for part in parts], axis=0)
        if pad > 3 * height:
            stacked = jnp.concatenate([stacked, jnp.zeros((pad - 3 * height, 2 * PC), F32)], axis=0)
        high, low = split(stacked)
        depth = [high, high, low]
        if deep > 3 * pad:
            depth.append(jnp.zeros((deep - 3 * pad, 2 * PC), BF16))
        along = jnp.dot(operator, jnp.concatenate(depth, axis=0), preferred_element_type=F32)
        store(pair, along, (0, 1))
        if pair == 0:
            store(pairs, along, (1, 0))

    def window(ref, start, count):
        size = 2 * height
        parts = []
        for k in range(bases):
            for move in (0, 1):
                parts.append(ref[k, (start + move) * size : (start + move + count) * size, :])
        return jnp.concatenate(parts, axis=1)

    def blocks(start, count, weights_ref):
        high = jnp.dot(window(high_ref, start, count), weights_ref[0], preferred_element_type=F32)
        low = jnp.dot(window(low_ref, start, count), weights_ref[0, :, :PC], preferred_element_type=F32)
        return high[:, :PC] + high[:, PC:] + low

    main = blocks(0, pairs, cols_ref)
    edge = blocks(pairs - 1, 1, edge_ref)[height:]
    turned = [None] * pieces
    for n in range(pieces):
        row = (2 * (n % pairs) + n // pairs) * height
        block = main[row : row + height] if n < pieces - 1 else edge
        turned[n] = pltpu.roll(block, PC // 2, 1)
    lane = lax.broadcasted_iota(jnp.int32, (height, PC), 1)

    if first == 0:
        @pl.when(step == 0)
        def _():
            acc_ref[...] = jnp.zeros_like(acc_ref)

    for c in range(pieces):
        piece = jnp.where(lane < PC // 2, turned[c - 1], turned[c])
        span = slice(c * PC, (c + 1) * PC)
        out_ref[0, :, span] = piece.astype(BF16)
        slot = slots_ref[visit * pieces + c]
        acc_ref[slot] += inv_ref[0, :, span] * piece

    @pl.when(step == pl.num_programs(0) - 1)
    def _():
        count = acc_ref.shape[0] // 2
        keep_ref[...] = acc_ref[:count]
        send_ref[...] = acc_ref[count:]


def scatter_sum(keep, send, size):
    bit = 1
    while bit < size:
        pairs = [(i, i ^ bit) for i in range(size)]
        keep = keep + lax.ppermute(send, "tile", pairs)
        bit *= 2
        if bit < size:
            count = keep.shape[0] // 2
            keep, send = keep[:count], keep[count:]
    return keep


def on_device(image, inv_var, shift, col_offset, psf_rows, psf_cols, placement):
    visits, height, width = image.shape
    bases, length = psf_rows.shape[1:]
    size = lax.axis_size("tile")
    if size & (size - 1) or length // 2 + 3 > height or width % (2 * PC):
        raise ValueError("unsupported sizes")
    me = lax.axis_index("tile")
    pieces = width // PC
    rising = [(i, i + 1) for i in range(size - 1)]
    above = lax.ppermute(image, "tile", rising)
    below = lax.ppermute(image, "tile", [(j, i) for i, j in rising])

    relative = placement.reshape(-1) ^ me
    slots = jnp.zeros_like(relative)
    bits = size.bit_length() - 1
    for b in range(bits):
        slots = slots | (((relative >> b) & 1) << (bits - 1 - b))
    wide = 2 * PC

    def lanes(x):
        return jnp.pad(x, ((0, 0), (0, 0), (0, wide - x.shape[2])))

    row_tap = tap_weights(shift[:, 0])
    col_tap = tap_weights(shift[:, 1])
    vecs = jnp.concatenate(
        [
            lanes(psf_rows[:, :, ::-1]),
            lanes(psf_cols),
            lanes(row_tap[:, None, ::-1]),
            lanes(col_tap[:, None, :]),
        ],
        axis=1,
    )
    rank = vecs.shape[1]
    scal = jnp.concatenate(
        [jnp.stack([me * height, jnp.int32(size * height)]).astype(jnp.int32), col_offset]
    )
    deep = round_up(3 * round_up(3 * height, 16), 128)
    smem = pl.BlockSpec(memory_space=pltpu.SMEM)

    def per_visit(*shape):
        return pl.BlockSpec((1,) + shape, lambda v: (v,) + (0,) * len(shape))

    def whole(*shape):
        return pl.BlockSpec(shape, lambda v: (0,) * len(shape))

    rows_op, cols_op, edge_op, den = pl.pallas_call(
        functools.partial(prepare_kernel, bases, length, height),
        grid=(visits,),
        in_specs=[smem, smem, per_visit(rank, wide), per_visit(height, width)],
        out_specs=[
            per_visit(bases * height, deep),
            per_visit(bases * wide, wide),
            per_visit(bases * wide, wide),
            whole(size, height, PC),
        ],
        out_shape=[
            jax.ShapeDtypeStruct((visits, bases * height, deep), BF16),
            jax.ShapeDtypeStruct((visits, bases * wide, wide), BF16),
            jax.ShapeDtypeStruct((visits, bases * wide, wide), BF16),
            jax.ShapeDtypeStruct((size, height, PC), F32),
        ],
        name="prepare",
        cost_estimate=pl.CostEstimate(
            flops=visits * 12 * wide * wide * bases * PC, bytes_accessed=4 * visits * height * width, transcendentals=0
        ),
    )(slots, scal, vecs, inv_var)
    denom = scatter_sum(den[: size // 2], den[size // 2 :], size)

    pair_rows = (pieces + 2) * height
    half = (size // 2, height, PC)
    matched, send, keep = pl.pallas_call(
        functools.partial(match_kernel, bases, 0, True),
        grid=(visits,),
        in_specs=[smem]
        + [per_visit(height, width)] * 4
        + [per_visit(bases * height, deep)]
        + [per_visit(bases * wide, wide)] * 2,
        out_specs=[per_visit(height, width), whole(*half), whole(*half)],
        out_shape=[
            jax.ShapeDtypeStruct((visits, height, width), BF16),
            jax.ShapeDtypeStruct(half, F32),
            jax.ShapeDtypeStruct(half, F32),
        ],
        scratch_shapes=[
            pltpu.VMEM((bases, pair_rows, PC), BF16),
            pltpu.VMEM((bases, pair_rows, PC), BF16),
            pltpu.VMEM((size, height, PC), F32),
        ],
        name="match",
        cost_estimate=pl.CostEstimate(
            flops=visits * 6 * bases * height * width * 256, bytes_accessed=20 * visits * height * width, transcendentals=0
        ),
    )(slots, above, image, below, inv_var, rows_op, cols_op, edge_op)
    numer = scatter_sum(keep, send, size)
    return matched, numer / jnp.maximum(denom, 1.0)


def solution(mesh):
    in_specs = (
        P(None, ("groups", "tile"), None),
        P(None, ("groups", "tile"), None),
        P("groups", None),
        P("groups"),
        P("groups", None, None),
        P("groups", None, None),
        P(("groups", "tile"), None),
    )
    out_specs = (P(None, ("groups", "tile"), None), P(("groups", "tile"), None, None))
    return jax.shard_map(
        on_device, mesh=mesh, in_specs=in_specs, out_specs=out_specs, check_vma=False
    )
```

time: 231 us -> 67.8 us (0.29)
  local copies, waits for them, and re-layouts: 99 us -> 4.93 us
  waiting for transfers between devices: 71 us -> 3.05 us
  starting transfers between devices: 13.7 us -> 36.1 us
  matrix products: 18.1 us -> 0 us
  Pallas kernels: 0 us -> 17.6 us
  between operations: 14.7 us -> 0.76 us
  other arithmetic: 13 us -> 4.97 us
    reduce_scatter x1 -> x0, waiting for transfers between devices: 71 us -> none  [on_device(): lax.psum_scatter(jnp.einsum('pvc,svrcx->psrx', onehot, stacked, precision...]
    gather x84 -> x0, local copies, waits for them, and re-layouts: 66.2 us -> none
    ppermute x4 -> x10, starting transfers between devices: 13.7 us -> 36.1 us  [the longest x8 32.3 us: scatter_sum(): keep = keep + lax.ppermute(send, 'tile', pairs)]
    dot_general x5 -> x0, matrix products: 18.1 us -> none  [the longest x1 8.64 us: on_device(): jnp.einsum('vkinw,vkow->vino', windows, col_band, precision=lax.Precision...]
    pallas_call x0 -> x2, Pallas kernels: none -> 17.6 us  [the longest x1 9.16 us: on_device(): pl.pallas_call(functools.partial(prepare_kernel, bases, length, height),...]
    unnamed x70 -> x8, local copies, waits for them, and re-layouts: 15.8 us -> 3.05 us
    add x4 -> x6, other arithmetic: 10 us -> 0.94 us  [scatter_sum(): keep = keep + lax.ppermute(send, 'tile', pairs)]
    eq x2 -> x0, local copies, waits for them, and re-layouts: 4.85 us -> none  [the longest x1 4.76 us: band_table(): index[:, :, None] == jnp.arange(41, dtype=jnp.int32)[None, None, :]]
  transfers between devices with their start and end apart: 5 -> 10, of which waited for: 1 -> 2; matrix products, arithmetic and copies ran while one was open for 9% -> 11% of each run, Pallas kernels for 0% -> 26%
where the time goes in v1:
time: 67.8 us; the launch traced here: 67.4 us
  starting transfers between devices  36.1 us (53%)
  Pallas kernels  17.6 us (26%)
  other arithmetic  4.97 us (7%)
  local copies, waits for them, and re-layouts  4.93 us (7%)
  waiting for transfers between devices  3.05 us (4%)
  between operations  0.76 us (1%)
    ppermute x8, starting transfers between devices, scatter_sum(): keep = keep + lax.ppermute(send, 'tile', pairs)  32.3 us
    pallas_call x1, Pallas kernels, on_device(): pl.pallas_call(functools.partial(prepare_kernel, bases, length, height),...  9.16 us
    pallas_call x1, Pallas kernels, on_device(): pl.pallas_call(functools.partial(match_kernel, bases, 0, True), grid=(vis...  8.47 us
    unnamed x8, local copies, waits for them, and re-layouts  3.05 us
    ppermute x8, waiting for transfers between devices, scatter_sum(): keep = keep + lax.ppermute(send, 'tile', pairs)  3.05 us
    ppermute x1, starting transfers between devices, on_device(): above = lax.ppermute(image, 'tile', rising)  2.5 us
  transfers between devices with their start and end apart: 10, of which 2 were waited for; matrix products, arithmetic and copies ran while one was open for 11% of the time, Pallas kernels for 26%

profile of v1, /device:TPU:0, one launch (start us, length us, event | category | flops | bytes accessed | tf_op | source)
XLA Modules:
  0.0 67.4 jit_solution(10877412250902372515)
XLA Ops:
  0.6 2.5 %collective-permute-start = (f32[4,24,4096]{2,1,0:T(8,128)}, f32[4,24,4096]{2,1,0:T(8,128)S(1)}, u32[]{:S(2)}, u32[]{:S(2)}) collective-permute-start(f32[4,24,4096]{2,1,0:T(8,128)} %own_ref.1), channel_id=1, source_target_pairs={{0,1},{1,2},{2,3},{3,4},{4,5},{5,6},{6,7},{7,8},{8,9},{9,10},{10,1... | collective-permute-start | bytes 4718600 | tf_op jit(solution)/shard_map/ppermute | solution.py:194
  3.1 1.3 %collective-permute-start.1 = (f32[4,24,4096]{2,1,0:T(8,128)}, f32[4,24,4096]{2,1,0:T(8,128)S(1)}, u32[]{:S(2)}, u32[]{:S(2)}) collective-permute-start(f32[4,24,4096]{2,1,0:T(8,128)} %own_ref.1), channel_id=1, source_target_pairs={{1,0},{2,1},{3,2},{4,3},{5,4},{6,5},{7,6},{8,7},{9,8},{10,9},{11,1... | collective-permute-start | bytes 4718600 | tf_op jit(solution)/shard_map/ppermute | solution.py:195
  4.5 0.8 %slice_bitcast_fusion = (f32[4]{0:T(128)S(1)}, f32[4]{0:T(128)S(1)}) fusion(f32[4,2]{0,1:T(2,128)} %param.10), kind=kLoop, calls=%fused_computation.134 | loop fusion | bytes 64 | tf_op jit(solution)/shard_map/add | solution.py:21
  5.2 0.2 fusion.77
  5.4 0.1 broadcast_divide_fusion.1
  5.6 0.1 rev.7
  5.7 0.7 %copy.9 = f32[4,3,41]{2,1,0:T(4,128)S(1)} copy(f32[4,3,41]{2,0,1:T(4,128)} %param.12) | data formatting | bytes 3936 | tf_op args[4]
  6.3 0.1 rev.6
  6.4 0.7 %copy.10 = f32[4,3,41]{2,1,0:T(4,128)S(1)} copy(f32[4,3,41]{2,0,1:T(4,128)} %param.13) | data formatting | bytes 3936 | tf_op args[5]
  7.1 1.3 %pad_add_fusion.scal_ref = s32[6]{0:T(128)} fusion(s32[4]{0:T(128)} %param.11, s32[1]{0:T(128)} %constant.18.clone.1, s32[1]{0:T(128)} %bitcast.1), kind=kLoop, calls=%fused_computation.132 | loop fusion | flops 12 | bytes 48 | tf_op jit(solution)/shard_map/concatenate | solution.py:219
  8.4 0.6 select_maximum_fusion.vecs_ref
  9.0 1.2 %or_bitcast_fusion.slots_ref = s32[128]{0:T(128)} fusion(s32[128,1]{0,1:T(1,128)} %param.14, s32[]{:T(128)S(6)} %axis_index.12), kind=kLoop, calls=%fused_computation.133 | loop fusion | flops 2048 | bytes 1028 | tf_op jit(solution)/shard_map/or | solution.py:201
  10.2 9.2 %prepare.1 = (bf16[4,72,256]{2,1,0:T(8,128)(2,1)}, bf16[4,768,256]{2,1,0:T(8,128)(2,1)}, bf16[4,768,256]{2,1,0:T(8,128)(2,1)}, f32[16,24,128]{2,1,0:T(8,128)}) custom-call(s32[128]{0:T(128)} %or_bitcast_fusion.slots_ref, s32[6]{0:T(128)} %pad_add_fusion.scal_ref, f32[4,8,256]{2,1,0:T(8,128)} %select_maximum_fusion.vecs_ref, f32[4,24,4096]{2,1,0:T(8,128)} %inv_ref.3), custom_call_target="tpu_custom_call" | custom-call | flops 1207959552 | bytes 1572864 | tf_op jit(solution)/shard_map/prepare/pallas_call | solution.py:231
  19.4 0.9 %slice.57 = f32[8,24,128]{2,1,0:T(8,128)S(1)} slice(f32[16,24,128]{2,1,0:T(8,128)} %get-tuple-element.16), slice={[8:16], [0:24], [0:128]} | slice | bytes 196608 | tf_op jit(solution)/shard_map/slice | solution.py:252
  20.3 3.2 %collective-permute-start.6 = (f32[8,24,128]{2,1,0:T(8,128)S(1)}, f32[8,24,128]{2,1,0:T(8,128)S(1)}, u32[]{:S(2)}, u32[]{:S(2)}) collective-permute-start(f32[8,24,128]{2,1,0:T(8,128)S(1)} %slice.57), channel_id=1, source_target_pairs={{0,1},{1,0},{2,3},{3,2},{4,5},{5,4},{6,7},{7,6},{8,9},{9,8},{10,11... | collective-permute-start | bytes 294920 | tf_op jit(solution)/shard_map/ppermute | solution.py:177
  23.4 0.0 collective-permute-done.up_ref
  23.4 0.0 copy-start
  23.4 0.0 collective-permute-done.1.down_ref
  23.4 0.0 copy-start.1
  23.5 1.1 %copy-done = f32[4,24,4096]{2,1,0:T(8,128)} copy-done((f32[4,24,4096]{2,1,0:T(8,128)}, f32[4,24,4096]{2,1,0:T(8,128)S(1)}, u32[]{:S(2)}) %copy-start) | copy-done | bytes 1572888
  24.6 0.5 copy-done.1
  25.1 0.0 copy-start.2
  25.1 8.5 %match.1 = (bf16[4,24,4096]{2,1,0:T(8,128)(2,1)}, f32[8,24,128]{2,1,0:T(8,128)}, f32[8,24,128]{2,1,0:T(8,128)}) custom-call(s32[128]{0:T(128)} %or_bitcast_fusion.slots_ref, f32[4,24,4096]{2,1,0:T(8,128)} %copy-done, f32[4,24,4096]{2,1,0:T(8,128)} %own_ref.1, f32[4,24,4096]{2,1,0:T(8,128)} %copy-done.1, f32[4,24,4096]{2,1,0:T(8,128)} %inv_ref.3, ...), custom_call_target="tpu_custom_call" | custom-call | flops 1811939328 | bytes 7864320 | tf_op jit(solution)/shard_map/match/pallas_call | solution.py:256
  33.6 16.8 %collective-permute-start.2 = (f32[8,24,128]{2,1,0:T(8,128)}, f32[8,24,128]{2,1,0:T(8,128)S(1)}, u32[]{:S(2)}, u32[]{:S(2)}) collective-permute-start(f32[8,24,128]{2,1,0:T(8,128)} %get-tuple-element.15), channel_id=1, source_target_pairs={{0,1},{1,0},{2,3},{3,2},{4,5},{5,4},{6,7},{7,6},{8,9},{9,8},{10,11... | collective-permute-start | bytes 294920 | tf_op jit(solution)/shard_map/ppermute | solution.py:177
  50.4 0.0 collective-permute-done.6
  50.4 0.0 copy-done.2
  50.4 2.4 %collective-permute-start.7 = (f32[4,24,128]{2,1,0:T(8,128)S(1)}, f32[4,24,128]{2,1,0:T(8,128)S(1)}, u32[]{:S(2)}, u32[]{:S(2)}) collective-permute-start(f32[4,24,128]{2,1,0:T(8,128)S(1)} %slice.71), channel_id=1, source_target_pairs={{0,2},{1,3},{2,0},{3,1},{4,6},{5,7},{6,4},{7,5},{8,10},{9,11},{10,... | collective-permute-start | bytes 147464 | tf_op jit(solution)/shard_map/ppermute | solution.py:177
  52.8 0.0 collective-permute-done.2
  52.8 0.9 %add.101 = f32[8,24,128]{2,1,0:T(8,128)S(1)} add(f32[8,24,128]{2,1,0:T(8,128)} %get-tuple-element.14, f32[8,24,128]{2,1,0:T(8,128)S(1)} %collective-permute-done.2) | non-fusion elementwise | flops 24576 | bytes 294912 | tf_op jit(solution)/shard_map/add | solution.py:177
  53.7 1.4 %collective-permute-start.3 = (f32[4,24,128]{2,1,0:T(8,128)S(1)}, f32[4,24,128]{2,1,0:T(8,128)S(1)}, u32[]{:S(2)}, u32[]{:S(2)}) collective-permute-start(f32[4,24,128]{2,1,0:T(8,128)S(1)} %slice.65), channel_id=1, source_target_pairs={{0,2},{1,3},{2,0},{3,1},{4,6},{5,7},{6,4},{7,5},{8,10},{9,11},{10,... | collective-permute-start | bytes 147464 | tf_op jit(solution)/shard_map/ppermute | solution.py:177
  55.1 0.0 collective-permute-done.7
  55.2 2.0 %collective-permute-start.8 = (f32[2,24,128]{2,1,0:T(8,128)S(1)}, f32[2,24,128]{2,1,0:T(8,128)S(1)}, u32[]{:S(2)}, u32[]{:S(2)}) collective-permute-start(f32[2,24,128]{2,1,0:T(8,128)S(1)} %slice.73), channel_id=1, source_target_pairs={{0,4},{1,5},{2,6},{3,7},{4,0},{5,1},{6,2},{7,3},{8,12},{9,13},{10,... | collective-permute-start | bytes 73736 | tf_op jit(solution)/shard_map/ppermute | solution.py:177
  57.2 0.7 collective-permute-done.3
  57.9 1.6 %collective-permute-start.4 = (f32[2,24,128]{2,1,0:T(8,128)S(1)}, f32[2,24,128]{2,1,0:T(8,128)S(1)}, u32[]{:S(2)}, u32[]{:S(2)}) collective-permute-start(f32[2,24,128]{2,1,0:T(8,128)S(1)} %slice.67), channel_id=1, source_target_pairs={{0,4},{1,5},{2,6},{3,7},{4,0},{5,1},{6,2},{7,3},{8,12},{9,13},{10,... | collective-permute-start | bytes 73736 | tf_op jit(solution)/shard_map/ppermute | solution.py:177
  59.5 0.0 collective-permute-done.8
  59.5 2.6 %collective-permute-start.9 = (f32[1,24,128]{2,1,0:T(8,128)S(1)}, f32[1,24,128]{2,1,0:T(8,128)S(1)}, u32[]{:S(2)}, u32[]{:S(2)}) collective-permute-start(f32[1,24,128]{2,1,0:T(8,128)S(1)} %slice.75), channel_id=1, source_target_pairs={{0,8},{1,9},{2,10},{3,11},{4,12},{5,13},{6,14},{7,15},{8,0},{9,1},... | collective-permute-start | bytes 36872 | tf_op jit(solution)/shard_map/ppermute | solution.py:177
  62.1 0.0 collective-permute-done.4
  62.1 2.3 %collective-permute-start.5 = (f32[1,24,128]{2,1,0:T(8,128)S(1)}, f32[1,24,128]{2,1,0:T(8,128)S(1)}, u32[]{:S(2)}, u32[]{:S(2)}) collective-permute-start(f32[1,24,128]{2,1,0:T(8,128)S(1)} %slice.69), channel_id=1, source_target_pairs={{0,8},{1,9},{2,10},{3,11},{4,12},{5,13},{6,14},{7,15},{8,0},{9,1},... | collective-permute-start | bytes 36872 | tf_op jit(solution)/shard_map/ppermute | solution.py:177
  64.4 0.0 collective-permute-done.9
  64.4 2.3 %collective-permute-done.5 = f32[1,24,128]{2,1,0:T(8,128)S(1)} collective-permute-done((f32[1,24,128]{2,1,0:T(8,128)S(1)}, f32[1,24,128]{2,1,0:T(8,128)S(1)}, u32[]{:S(2)}, u32[]{:S(2)}) %collective-permute-start.5) | collective-permute-done | bytes 12320 | tf_op jit(solution)/shard_map/ppermute | solution.py:177
  66.8 0.6 fusion.3
  (12 shorter events, 0.1 us)
Async XLA Ops:
  0.6 22.8 %collective-permute-start = (f32[4,24,4096]{2,1,0:T(8,128)}, f32[4,24,4096]{2,1,0:T(8,128)S(1)}, u32[]{:S(2)}, u32[]{:S(2)}) collective-permute-start(f32[4,24,4096]{2,1,0:T(8,128)} %own_ref.1), channel_id=1, source_target_pairs={{0,1},{1,2},{2,3},{3,4},{4,5},{5,6},{6,7},{7,8},{8,9},{9,10},{10,1... | collective-permute-start | bytes 4718600 | tf_op jit(solution)/shard_map/ppermute | solution.py:194
  3.1 20.3 %collective-permute-start.1 = (f32[4,24,4096]{2,1,0:T(8,128)}, f32[4,24,4096]{2,1,0:T(8,128)S(1)}, u32[]{:S(2)}, u32[]{:S(2)}) collective-permute-start(f32[4,24,4096]{2,1,0:T(8,128)} %own_ref.1), channel_id=1, source_target_pairs={{1,0},{2,1},{3,2},{4,3},{5,4},{6,5},{7,6},{8,7},{9,8},{10,9},{11,1... | collective-permute-start | bytes 4718600 | tf_op jit(solution)/shard_map/ppermute | solution.py:195
  20.3 30.1 %collective-permute-start.6 = (f32[8,24,128]{2,1,0:T(8,128)S(1)}, f32[8,24,128]{2,1,0:T(8,128)S(1)}, u32[]{:S(2)}, u32[]{:S(2)}) collective-permute-start(f32[8,24,128]{2,1,0:T(8,128)S(1)} %slice.57), channel_id=1, source_target_pairs={{0,1},{1,0},{2,3},{3,2},{4,5},{5,4},{6,7},{7,6},{8,9},{9,8},{10,11... | collective-permute-start | bytes 294920 | tf_op jit(solution)/shard_map/ppermute | solution.py:177
  23.4 1.1 %copy-start = (f32[4,24,4096]{2,1,0:T(8,128)}, f32[4,24,4096]{2,1,0:T(8,128)S(1)}, u32[]{:S(2)}) copy-start(f32[4,24,4096]{2,1,0:T(8,128)S(1)} %collective-permute-done.up_ref) | copy-start | bytes 4718596
  23.4 1.7 %copy-start.1 = (f32[4,24,4096]{2,1,0:T(8,128)}, f32[4,24,4096]{2,1,0:T(8,128)S(1)}, u32[]{:S(2)}) copy-start(f32[4,24,4096]{2,1,0:T(8,128)S(1)} %collective-permute-done.1.down_ref) | copy-start | bytes 4718596
  25.1 25.3 %copy-start.2 = (f32[16,24,128]{2,1,0:T(8,128)S(1)}, f32[16,24,128]{2,1,0:T(8,128)}, u32[]{:S(2)}) copy-start(f32[16,24,128]{2,1,0:T(8,128)} %get-tuple-element.16) | copy-start | bytes 589828
  33.6 19.2 %collective-permute-start.2 = (f32[8,24,128]{2,1,0:T(8,128)}, f32[8,24,128]{2,1,0:T(8,128)S(1)}, u32[]{:S(2)}, u32[]{:S(2)}) collective-permute-start(f32[8,24,128]{2,1,0:T(8,128)} %get-tuple-element.15), channel_id=1, source_target_pairs={{0,1},{1,0},{2,3},{3,2},{4,5},{5,4},{6,7},{7,6},{8,9},{9,8},{10,11... | collective-permute-start | bytes 294920 | tf_op jit(solution)/shard_map/ppermute | solution.py:177
  50.4 4.7 %collective-permute-start.7 = (f32[4,24,128]{2,1,0:T(8,128)S(1)}, f32[4,24,128]{2,1,0:T(8,128)S(1)}, u32[]{:S(2)}, u32[]{:S(2)}) collective-permute-start(f32[4,24,128]{2,1,0:T(8,128)S(1)} %slice.71), channel_id=1, source_target_pairs={{0,2},{1,3},{2,0},{3,1},{4,6},{5,7},{6,4},{7,5},{8,10},{9,11},{10,... | collective-permute-start | bytes 147464 | tf_op jit(solution)/shard_map/ppermute | solution.py:177
  53.7 4.2 %collective-permute-start.3 = (f32[4,24,128]{2,1,0:T(8,128)S(1)}, f32[4,24,128]{2,1,0:T(8,128)S(1)}, u32[]{:S(2)}, u32[]{:S(2)}) collective-permute-start(f32[4,24,128]{2,1,0:T(8,128)S(1)} %slice.65), channel_id=1, source_target_pairs={{0,2},{1,3},{2,0},{3,1},{4,6},{5,7},{6,4},{7,5},{8,10},{9,11},{10,... | collective-permute-start | bytes 147464 | tf_op jit(solution)/shard_map/ppermute | solution.py:177
  55.2 4.3 %collective-permute-start.8 = (f32[2,24,128]{2,1,0:T(8,128)S(1)}, f32[2,24,128]{2,1,0:T(8,128)S(1)}, u32[]{:S(2)}, u32[]{:S(2)}) collective-permute-start(f32[2,24,128]{2,1,0:T(8,128)S(1)} %slice.73), channel_id=1, source_target_pairs={{0,4},{1,5},{2,6},{3,7},{4,0},{5,1},{6,2},{7,3},{8,12},{9,13},{10,... | collective-permute-start | bytes 73736 | tf_op jit(solution)/shard_map/ppermute | solution.py:177
  57.9 4.2 %collective-permute-start.4 = (f32[2,24,128]{2,1,0:T(8,128)S(1)}, f32[2,24,128]{2,1,0:T(8,128)S(1)}, u32[]{:S(2)}, u32[]{:S(2)}) collective-permute-start(f32[2,24,128]{2,1,0:T(8,128)S(1)} %slice.67), channel_id=1, source_target_pairs={{0,4},{1,5},{2,6},{3,7},{4,0},{5,1},{6,2},{7,3},{8,12},{9,13},{10,... | collective-permute-start | bytes 73736 | tf_op jit(solution)/shard_map/ppermute | solution.py:177
  59.5 4.9 %collective-permute-start.9 = (f32[1,24,128]{2,1,0:T(8,128)S(1)}, f32[1,24,128]{2,1,0:T(8,128)S(1)}, u32[]{:S(2)}, u32[]{:S(2)}) collective-permute-start(f32[1,24,128]{2,1,0:T(8,128)S(1)} %slice.75), channel_id=1, source_target_pairs={{0,8},{1,9},{2,10},{3,11},{4,12},{5,13},{6,14},{7,15},{8,0},{9,1},... | collective-permute-start | bytes 36872 | tf_op jit(solution)/shard_map/ppermute | solution.py:177
  62.1 4.7 %collective-permute-start.5 = (f32[1,24,128]{2,1,0:T(8,128)S(1)}, f32[1,24,128]{2,1,0:T(8,128)S(1)}, u32[]{:S(2)}, u32[]{:S(2)}) collective-permute-start(f32[1,24,128]{2,1,0:T(8,128)S(1)} %slice.69), channel_id=1, source_target_pairs={{0,8},{1,9},{2,10},{3,11},{4,12},{5,13},{6,14},{7,15},{8,0},{9,1},... | collective-permute-start | bytes 36872 | tf_op jit(solution)/shard_map/ppermute | solution.py:177

commit v2 on v0

v2 whole, which is shorter than its diff:
```python
import functools
import math
import jax
import jax.numpy as jnp
from jax import lax
from jax.experimental import pallas as pl
from jax.experimental.pallas import tpu as pltpu
from jax.sharding import PartitionSpec as P

PC = 128
WIDE = 2 * PC
TAPS = 3
F32 = jnp.float32
BF16 = jnp.bfloat16
HIGHEST = lax.Precision.HIGHEST
GRANT = 24 * 1024 * 1024


def round_up(number, unit):
    return -(-number // unit) * unit


def split(x):
    high = x.astype(BF16)
    low = (x - high.astype(F32)).astype(BF16)
    return high, low


def lane_of(shape):
    return lax.broadcasted_iota(jnp.int32, shape, len(shape) - 1)


def row_of(shape):
    return lax.broadcasted_iota(jnp.int32, shape, 0)


def sinc(u):
    angle = math.pi * u
    return jnp.where(u == 0.0, 1.0, jnp.sin(angle) / jnp.where(u == 0.0, 1.0, angle))


def tap_lanes(shift_ref):
    visits = shift_ref.shape[1]
    rows = round_up(2 * visits, 8)
    row, lane = row_of((rows, PC)), lane_of((rows, PC))
    fraction = jnp.zeros((rows, PC), F32)
    for r in range(2 * visits):
        fraction = jnp.where(row == r, shift_ref[r % 2, r // 2], fraction)
    u = (lane - TAPS).astype(F32) + fraction
    weight = jnp.where(jnp.abs(u) < 3.0, sinc(u) * sinc(u / 3.0), 0.0)
    weight = jnp.where(lane < 2 * TAPS + 1, weight, 0.0)
    return weight / jnp.sum(weight, axis=1, keepdims=True)


def band(vector, shift, rows=PC):
    wide = vector.shape[-1]
    turned = pltpu.roll(jnp.broadcast_to(vector, (8, wide)), shift, 1)[:1]
    full = jnp.broadcast_to(turned, (rows, wide))
    return pltpu.roll(full, 0, 1, stride=1, stride_axis=0)


def padded(block, rows, lanes):
    high, wide = block.shape
    block = jnp.concatenate([block, jnp.zeros((high, lanes - wide), F32)], axis=1)
    return jnp.concatenate([block, jnp.zeros((rows - high, lanes), F32)], axis=0)


def weights_kernel(order, place_ref, me_ref, inv_ref, keep_ref, send_ref, den_ref):
    visits, _, width = inv_ref.shape
    pieces = width // PC
    den_ref[...] = jnp.zeros_like(den_ref)
    for n in range(visits * pieces):
        slot = place_ref[n] ^ me_ref[0]
        span = slice(n % pieces * PC, (n % pieces + 1) * PC)
        den_ref[slot] += inv_ref[n // pieces, :, span]
    hand_out(order, den_ref, keep_ref, send_ref)


def hand_out(order, acc_ref, keep_ref, send_ref):
    half = len(order) // 2
    for i, slot in enumerate(order):
        if i < half:
            keep_ref[i, : acc_ref.shape[1]] = acc_ref[slot]
        else:
            send_ref[i - half] = acc_ref[slot]


def prepare_kernel(
    height, size, me_ref, shift_ref, offset_ref, psf_rows_ref, psf_cols_ref, rows_ref, cols_ref, edge_ref
):
    bases, visits, length = psf_rows_ref.shape
    half = length // 2
    ext = 3 * height
    pad = round_up(ext, 16)
    all_taps = tap_lanes(shift_ref)
    lane, row = lane_of((PC, PC)), row_of((PC, PC))
    left = lane < PC // 2
    place = lane + me_ref[0] * height - height
    inside = (place >= 0) & (place < size * height)
    for visit in range(visits):
        warp = jnp.where(inside, band(all_taps[2 * visit : 2 * visit + 1], PC - TAPS), 0.0)
        kernels = padded(psf_rows_ref[:, visit, :], 8, PC)
        psf = jnp.zeros((PC, PC), F32)
        for k in range(bases):
            one = jnp.where(lane < height, band(kernels[k : k + 1], PC - (height + half)), 0.0)
            psf = psf + (pltpu.roll(one, k * height, 1) if k else one)
        rows = jnp.dot(warp, psf, precision=HIGHEST, preferred_element_type=F32)
        rows = jnp.where(row < ext, rows, 0.0).T[: bases * height]
        high = rows.astype(BF16).astype(F32)
        low = rows - high
        blank = jnp.zeros_like(rows)
        high = jnp.concatenate([high, blank], axis=1)
        low = jnp.concatenate([low, blank], axis=1)
        rows_ref[visit] = (high + pltpu.roll(low, pad, 1) + pltpu.roll(high, 2 * pad, 1)).astype(BF16)
        taps = all_taps[2 * visit + 1 : 2 * visit + 2]
        offset = offset_ref[visit]
        kernels = padded(psf_cols_ref[:, visit, :], 8, PC)
        joined = jnp.zeros((8, PC), F32)
        for t in range(2 * TAPS + 1):
            weight = jnp.sum(jnp.where(lane[:8] == t, taps, 0.0), axis=1, keepdims=True)
            joined = joined + weight * pltpu.roll(kernels, (t - TAPS) % PC, 1)
        start = PC // 2 - half
        ends = []
        for k in range(bases):
            both = band(joined[k : k + 1], start + offset)
            for part, at in ((jnp.where(lane < row, both, 0.0), 0), (jnp.where(lane > row, both, 0.0), PC)):
                high, low = split(part)
                span = slice(k * WIDE + at, k * WIDE + at + PC)
                cols_ref[visit, span, :PC] = high
                cols_ref[visit, span, PC:] = low
            ends.append(jnp.where(left == (lane < row), band(kernels[k : k + 1], start), 0.0))
        far = jnp.concatenate([taps, jnp.zeros_like(taps)], axis=1)
        warp = band(far, lax.rem(offset + WIDE - TAPS, WIDE))[:, :PC]
        both = jnp.dot(warp, jnp.concatenate(ends, axis=1), precision=HIGHEST, preferred_element_type=F32)
        for k in range(bases):
            part = both[:, k * PC : (k + 1) * PC]
            for part, at in ((jnp.where(left, part, 0.0), 0), (jnp.where(left, 0.0, part), PC)):
                high, low = split(part)
                span = slice(k * WIDE + at, k * WIDE + at + PC)
                edge_ref[visit, span, :PC] = high
                edge_ref[visit, span, PC:] = low


def match_kernel(
    bases, first, last, order, place_ref, me_ref, fore_ref, back_ref, image_ref, inv_ref, rows_ref, cols_ref,
    edge_ref, *refs
):
    if first:
        old_ref, _, *refs = refs
    if last:
        mine_ref, other_ref, out_ref, keep_ref, send_ref, high_ref, low_ref, acc_ref = refs
    else:
        out_ref, acc_ref, high_ref, low_ref = refs
    step = pl.program_id(0)
    visit = step + first
    height, width = image_ref.shape[1:]
    pieces = width // PC
    pairs = pieces // 2
    pad = round_up(3 * height, 16)
    deep = rows_ref.shape[2]
    operator = rows_ref[visit]

    def column(n):
        span = slice(n * PC, (n + 1) * PC)
        parts = [fore_ref[step, :, span], image_ref[visit, :, span], back_ref[step, :, span]]
        if pad > 3 * height:
            parts.append(jnp.zeros((pad - 3 * height, PC), F32))
        return jnp.concatenate(parts, axis=0)

    def store(pair, along, turn):
        for k in range(bases):
            block = [along[k * height : (k + 1) * height, h * PC : (h + 1) * PC] for h in turn]
            high, low = split(jnp.concatenate(block, axis=0))
            high_ref[k, pair * 2 * height : (pair + 1) * 2 * height, :] = high
            low_ref[k, pair * 2 * height : (pair + 1) * 2 * height, :] = low

    for pair in range(pairs):
        stacked = jnp.concatenate([column(pair), column(pair + pairs)], axis=1)
        high, low = split(stacked)
        depth = [high, high, low]
        if deep > 3 * pad:
            depth.append(jnp.zeros((deep - 3 * pad, WIDE), BF16))
        along = jnp.dot(operator, jnp.concatenate(depth, axis=0), preferred_element_type=F32)
        store(pair, along, (0, 1))
        if pair == 0:
            store(pairs, along, (1, 0))

    def window(ref, start, count):
        size = 2 * height
        parts = []
        for k in range(bases):
            for move in (0, 1):
                parts.append(ref[k, (start + move) * size : (start + move + count) * size, :])
        return jnp.concatenate(parts, axis=1)

    def blocks(start, count, ref):
        high = jnp.dot(window(high_ref, start, count), ref[visit], preferred_element_type=F32)
        low = jnp.dot(window(low_ref, start, count), ref[visit, :, :PC], preferred_element_type=F32)
        return high[:, :PC] + high[:, PC:] + low

    main = blocks(0, pairs, cols_ref)
    edge = blocks(pairs - 1, 1, edge_ref)[height:]
    turned = [None] * pieces
    for n in range(pieces):
        row = (2 * (n % pairs) + n // pairs) * height
        block = main[row : row + height] if n < pieces - 1 else edge
        turned[n] = pltpu.roll(block, PC // 2, 1)
    lane = lane_of((height, PC))

    @pl.when(step == 0)
    def _():
        acc_ref[...] = old_ref[...] if first else jnp.zeros_like(acc_ref)

    for c in range(pieces):
        piece = jnp.where(lane < PC // 2, turned[c - 1], turned[c])
        span = slice(c * PC, (c + 1) * PC)
        out_ref[0, :, span] = piece.astype(BF16)
        slot = place_ref[visit * pieces + c] ^ me_ref[0]
        acc_ref[slot] += inv_ref[visit, :, span] * piece

    if last:
        @pl.when(step == pl.num_programs(0) - 1)
        def _():
            hand_out(order, acc_ref, keep_ref, send_ref)
            keep_ref[:, height:] = mine_ref[...] + other_ref[...]


def exchange(send, size, bit):
    return lax.ppermute(send, "tile", [(i, i ^ bit) for i in range(size)])


def on_device(image, inv_var, shift, col_offset, psf_rows, psf_cols, placement):
    visits, height, width = image.shape
    bases, length = psf_rows.shape[1:]
    size = lax.axis_size("tile")
    reach = length // 2 + TAPS
    if size & (size - 1) or reach > height or height % 8 or width % WIDE or visits < 3:
        raise ValueError("unsupported sizes")
    me = lax.axis_index("tile").astype(jnp.int32).reshape(1)
    place = placement.reshape(-1)
    bits = [1 << b for b in range(size.bit_length() - 1)]
    order = [0]
    for bit in reversed(bits):
        order = order + [slot ^ bit for slot in order]
    order = tuple(order)
    rising = [(i, i + 1) for i in range(size - 1)]
    falling = [(j, i) for i, j in rising]
    smem = pl.BlockSpec(memory_space=pltpu.SMEM)
    vmem = pl.BlockSpec(memory_space=pltpu.VMEM)
    anywhere = pl.BlockSpec(memory_space=pl.ANY)
    params = pltpu.CompilerParams(vmem_limit_bytes=GRANT)
    chunks = ((0, visits - 2), (visits - 2, 1), (visits - 1, 1))

    halos = []
    for (first, count) in chunks:
        part = image[first : first + count]
        fore = lax.ppermute(part, "tile", rising)
        back = lax.ppermute(part, "tile", falling)
        halos.append((fore, back))

    half = jax.ShapeDtypeStruct((size // 2, height, PC), F32)
    sums = pltpu.VMEM((size, height, PC), F32)
    weights = pl.pallas_call(
        functools.partial(weights_kernel, order),
        in_specs=[smem, smem, vmem],
        out_specs=[vmem, vmem],
        out_shape=[half, half],
        scratch_shapes=[sums],
        compiler_params=params,
        name="weights",
    )
    den = weights(place, me, inv_var)
    denom = (den[0], exchange(den[1], size, bits[0]))

    deep = round_up(3 * round_up(3 * height, 16), 128)
    prepare = pl.pallas_call(
        functools.partial(prepare_kernel, height, size),
        in_specs=[smem, smem, smem, vmem, vmem],
        out_specs=[vmem] * 3,
        out_shape=[
            jax.ShapeDtypeStruct((visits, bases * height, deep), BF16),
            jax.ShapeDtypeStruct((visits, bases * WIDE, WIDE), BF16),
            jax.ShapeDtypeStruct((visits, bases * WIDE, WIDE), BF16),
        ],
        compiler_params=params,
        name="prepare",
    )
    operators = prepare(
        me, shift.T, col_offset, psf_rows.transpose(1, 0, 2), psf_cols.transpose(1, 0, 2)
    )

    carried = ()
    for (first, count), (fore, back) in zip(chunks, halos):
        last = first + count == visits
        shapes = [jax.ShapeDtypeStruct((visits, height, width), BF16)]
        specs = [pl.BlockSpec((1, height, width), lambda v, first=first: (v + first, 0, 0))]
        pair_rows = (width // PC + 2) * height
        scratch = [pltpu.VMEM((bases, pair_rows, PC), BF16)] * 2
        inputs = [vmem] * 7
        extra = []
        if first:
            inputs += [vmem, anywhere]
            extra += [carried[1], carried[0]]
        if last:
            inputs += [vmem, vmem]
            extra += denom
            shapes += [jax.ShapeDtypeStruct((size // 2, 2 * height, PC), F32), half]
            specs += [vmem, vmem]
            scratch += [sums]
        else:
            shapes += [jax.ShapeDtypeStruct((size, height, PC), F32)]
            specs += [vmem]
        match = pl.pallas_call(
            functools.partial(match_kernel, bases, first, last, order),
            grid=(count,),
            in_specs=[smem, smem] + inputs,
            out_specs=specs,
            out_shape=shapes,
            scratch_shapes=scratch,
            input_output_aliases={10: 0} if first else {},
            compiler_params=params,
            cost_estimate=pl.CostEstimate(
                flops=count * 6 * bases * height * width * WIDE,
                bytes_accessed=20 * count * height * width,
                transcendentals=0,
            ),
        )
        carried = match(place, me, fore, back, image, inv_var, *operators, *extra)
    matched, keep, send = carried
    received = exchange(send, size, bits[0])
    keep = jnp.concatenate([keep[:, :height] + received, keep[:, height:]], axis=1)
    for bit in bits[1:]:
        count = keep.shape[0] // 2
        keep = keep[:count] + exchange(keep[count:], size, bit)
    return matched, keep[:, :height] / jnp.maximum(keep[:, height:], 1.0)


def solution(mesh):
    in_specs = (
        P(None, ("groups", "tile"), None),
        P(None, ("groups", "tile"), None),
        P("groups", None),
        P("groups"),
        P("groups", None, None),
        P("groups", None, None),
        P(("groups", "tile"), None),
    )
    out_specs = (P(None, ("groups", "tile"), None), P(("groups", "tile"), None, None))

    return jax.shard_map(
        on_device, mesh=mesh, in_specs=in_specs, out_specs=out_specs, check_vma=False
    )
```

time: 231 us -> 72.6 us (0.31)
  local copies, waits for them, and re-layouts: 99 us -> 5.47 us
  waiting for transfers between devices: 71 us -> 9.01 us
  starting transfers between devices: 13.7 us -> 39.4 us
  matrix products: 18.1 us -> 0 us
  Pallas kernels: 0 us -> 16.8 us
  between operations: 14.7 us -> 0.83 us
  other arithmetic: 13 us -> 0.66 us
    reduce_scatter x1 -> x0, waiting for transfers between devices: 71 us -> none  [on_device(): lax.psum_scatter(jnp.einsum('pvc,svrcx->psrx', onehot, stacked, precision...]
    gather x84 -> x0, local copies, waits for them, and re-layouts: 66.2 us -> none
    ppermute x4 -> x11, starting transfers between devices: 13.7 us -> 39.4 us  [the longest x5 23.6 us: exchange(): return lax.ppermute(send, 'tile', [(i, i ^ bit) for i in range(size)])]
    dot_general x5 -> x0, matrix products: 18.1 us -> none  [the longest x1 8.64 us: on_device(): jnp.einsum('vkinw,vkow->vino', windows, col_band, precision=lax.Precision...]
    pallas_call x0 -> x5, Pallas kernels: none -> 16.8 us  [the longest x3 10.9 us: on_device(): carried = match(place, me, fore, back, image, inv_var, *operators, *extra)]
    unnamed x70 -> x18, local copies, waits for them, and re-layouts: 15.8 us -> 2.3 us
    add x4, other arithmetic: 10 us -> 0.04 us  [the longest x3 0.02 us: on_device(): keep = keep[:count] + exchange(keep[count:], size, bit)]
    ppermute x4 -> x11, waiting for transfers between devices: 0.01 us -> 9.01 us  [the longest x5 9 us: exchange(): return lax.ppermute(send, 'tile', [(i, i ^ bit) for i in range(size)])]
  transfers between devices with their start and end apart: 5 -> 11, of which waited for: 1 -> 4; matrix products, arithmetic and copies ran while one was open for 9% -> 1% of each run, Pallas kernels for 0% -> 19%
where the time goes in v2:
time: 72.6 us; the launch traced here: 72.2 us
  starting transfers between devices  39.4 us (54%)
  Pallas kernels  16.8 us (23%)
  waiting for transfers between devices  9.01 us (12%)
  local copies, waits for them, and re-layouts  5.47 us (8%)
  between operations  0.83 us (1%)
    ppermute x5, starting transfers between devices, exchange(): return lax.ppermute(send, 'tile', [(i, i ^ bit) for i in range(size)])  23.6 us
    ppermute x3, starting transfers between devices, on_device(): fore = lax.ppermute(part, 'tile', rising)  12 us
    pallas_call x3, Pallas kernels, on_device(): carried = match(place, me, fore, back, image, inv_var, *operators, *extra)  10.9 us
    ppermute x5, waiting for transfers between devices, exchange(): return lax.ppermute(send, 'tile', [(i, i ^ bit) for i in range(size)])  9 us
    pallas_call x1, Pallas kernels, on_device(): prepare(me, shift.T, col_offset, psf_rows.transpose(1, 0, 2), psf_cols.tr...  4.78 us
    ppermute x3, starting transfers between devices, on_device(): back = lax.ppermute(part, 'tile', falling)  3.85 us
    slice x2, local copies, waits for them, and re-layouts, on_device(): part = image[first:first + count]  3.16 us
    unnamed x18, local copies, waits for them, and re-layouts  2.3 us
  transfers between devices with their start and end apart: 11, of which 4 were waited for; matrix products, arithmetic and copies ran while one was open for 1% of the time, Pallas kernels for 19%

profile of v2, /device:TPU:0, one launch (start us, length us, event | category | flops | bytes accessed | tf_op | source)
XLA Modules:
  0.0 72.2 jit_solution(4994682941588328808)
XLA Ops:
  0.6 0.0 copy-start
  0.6 0.0 copy-start.4
  0.6 0.0 copy-start.1
  0.7 2.2 %slice.41 = f32[2,24,4096]{2,1,0:T(8,128)} slice(f32[4,24,4096]{2,1,0:T(8,128)} %image_ref.5), slice={[0:2], [0:24], [0:4096]} | slice | bytes 1572864 | tf_op jit(solution)/shard_map/slice | solution.py:256
  2.9 0.0 copy-start.5
  2.9 0.0 copy-start.7
  2.9 2.6 %collective-permute-start.4 = (f32[2,24,4096]{2,1,0:T(8,128)}, f32[2,24,4096]{2,1,0:T(8,128)S(1)}, u32[]{:S(2)}, u32[]{:S(2)}) collective-permute-start(f32[2,24,4096]{2,1,0:T(8,128)} %slice.41), channel_id=1, source_target_pairs={{0,1},{1,2},{2,3},{3,4},{4,5},{5,6},{6,7},{7,8},{8,9},{9,10},{10,1... | collective-permute-start | bytes 2359304 | tf_op jit(solution)/shard_map/ppermute | solution.py:257
  5.5 1.3 %collective-permute-start.5 = (f32[2,24,4096]{2,1,0:T(8,128)}, f32[2,24,4096]{2,1,0:T(8,128)}, u32[]{:S(2)}, u32[]{:S(2)}) collective-permute-start(f32[2,24,4096]{2,1,0:T(8,128)} %slice.41), channel_id=1, source_target_pairs={{1,0},{2,1},{3,2},{4,3},{5,4},{6,5},{7,6},{8,7},{9,8},{10,9},{11,1... | collective-permute-start | bytes 2359304 | tf_op jit(solution)/shard_map/ppermute | solution.py:258
  6.8 0.0 copy-done
  6.8 0.9 %fusion.3 = (f32[1,24,4096]{2,1,0:T(8,128)}, f32[1,24,4096]{2,1,0:T(8,128)}) fusion(f32[4,24,4096]{2,1,0:T(8,128)S(1)} %copy-done), kind=kLoop, calls=%fused_computation.10 | loop fusion | bytes 1572864 | tf_op jit(solution)/shard_map/slice | solution.py:256
  7.7 5.8 %collective-permute-start.2 = (f32[1,24,4096]{2,1,0:T(8,128)}, f32[1,24,4096]{2,1,0:T(8,128)}, u32[]{:S(2)}, u32[]{:S(2)}) collective-permute-start(f32[1,24,4096]{2,1,0:T(8,128)} %get-tuple-element.26), channel_id=1, source_target_pairs={{0,1},{1,2},{2,3},{3,4},{4,5},{5,6},{6,7},{7,8},{8,9},{9,10},{10,1... | collective-permute-start | bytes 1179656 | tf_op jit(solution)/shard_map/ppermute | solution.py:257
  13.5 1.3 %collective-permute-start.3 = (f32[1,24,4096]{2,1,0:T(8,128)}, f32[1,24,4096]{2,1,0:T(8,128)}, u32[]{:S(2)}, u32[]{:S(2)}) collective-permute-start(f32[1,24,4096]{2,1,0:T(8,128)} %get-tuple-element.26), channel_id=1, source_target_pairs={{1,0},{2,1},{3,2},{4,3},{5,4},{6,5},{7,6},{8,7},{9,8},{10,9},{11,1... | collective-permute-start | bytes 1179656 | tf_op jit(solution)/shard_map/ppermute | solution.py:258
  14.8 3.6 %collective-permute-start = (f32[1,24,4096]{2,1,0:T(8,128)}, f32[1,24,4096]{2,1,0:T(8,128)S(1)}, u32[]{:S(2)}, u32[]{:S(2)}) collective-permute-start(f32[1,24,4096]{2,1,0:T(8,128)} %get-tuple-element.27), channel_id=1, source_target_pairs={{0,1},{1,2},{2,3},{3,4},{4,5},{5,6},{6,7},{7,8},{8,9},{9,10},{10,1... | collective-permute-start | bytes 1179656 | tf_op jit(solution)/shard_map/ppermute | solution.py:257
  18.4 0.0 collective-permute-done.4.fore_ref
  18.4 0.0 copy-start.2
  18.4 0.9 %copy-done.2 = f32[2,24,4096]{2,1,0:T(8,128)} copy-done((f32[2,24,4096]{2,1,0:T(8,128)}, f32[2,24,4096]{2,1,0:T(8,128)S(1)}, u32[]{:S(2)}) %copy-start.2) | copy-done | bytes 786456
  19.4 1.3 %collective-permute-start.1 = (f32[1,24,4096]{2,1,0:T(8,128)}, f32[1,24,4096]{2,1,0:T(8,128)}, u32[]{:S(2)}, u32[]{:S(2)}) collective-permute-start(f32[1,24,4096]{2,1,0:T(8,128)} %get-tuple-element.27), channel_id=1, source_target_pairs={{1,0},{2,1},{3,2},{4,3},{5,4},{6,5},{7,6},{8,7},{9,8},{10,9},{11,1... | collective-permute-start | bytes 1179656 | tf_op jit(solution)/shard_map/ppermute | solution.py:258
  20.7 0.0 copy-start.3
  20.7 0.0 copy-done.4
  20.7 0.0 copy-done.1
  20.7 1.1 %weights.1 = (f32[8,24,128]{2,1,0:T(8,128)S(1)}, f32[8,24,128]{2,1,0:T(8,128)S(1)}) custom-call(s32[128]{0:T(128)S(1)} %bitcast.5, s32[1]{0:T(128)} %bitcast.1.me_ref, f32[4,24,4096]{2,1,0:T(8,128)S(1)} %copy-done.1), custom_call_target="tpu_custom_call" | custom-call | tf_op jit(solution)/shard_map/weights/pallas_call | solution.py:272
  21.8 0.0 copy-done.5
  21.8 0.0 copy-done.7
  21.8 0.0 copy-start.6
  21.8 0.7 copy-done.6
  22.5 0.0 copy-start.8
  22.5 0.7 copy-done.8
  23.2 4.8 %prepare.1 = (bf16[4,72,256]{2,1,0:T(8,128)(2,1)S(1)}, bf16[4,768,256]{2,1,0:T(8,128)(2,1)S(1)}, bf16[4,768,256]{2,1,0:T(8,128)(2,1)S(1)}) custom-call(s32[1]{0:T(128)} %bitcast.1.me_ref, f32[2,4]{1,0:T(2,128)S(1)} %bitcast.11, s32[4]{0:T(128)S(1)} %copy-done.8, f32[3,4,41]{2,1,0:T(4,128)S(1)} %bitcast.9, f32[3,4,41]{2,1,0:T(4,128)S(1)} %bitcast.10), custom_call_target="tpu_custom_call" | custom-call | tf_op jit(solution)/shard_map/prepare/pallas_call | solution.py:288
  28.0 0.0 collective-permute-done.5.back_ref
  28.0 16.4 %collective-permute-start.6 = (f32[8,24,128]{2,1,0:T(8,128)S(1)}, f32[8,24,128]{2,1,0:T(8,128)S(1)}, u32[]{:S(2)}, u32[]{:S(2)}) collective-permute-start(f32[8,24,128]{2,1,0:T(8,128)S(1)} %get-tuple-element.22), channel_id=1, source_target_pairs={{0,1},{1,0},{2,3},{3,2},{4,5},{5,4},{6,7},{7,6},{8,9},{9,8},{10,11... | collective-permute-start | bytes 294920 | tf_op jit(solution)/shard_map/ppermute | solution.py:229
  44.3 0.0 copy-done.3
  44.3 4.7 %shard_map.86 = (bf16[4,24,4096]{2,1,0:T(8,128)(2,1)}, f32[16,24,128]{2,1,0:T(8,128)S(1)}) custom-call(s32[128]{0:T(128)S(1)} %bitcast.6, s32[1]{0:T(128)} %bitcast.1.me_ref, f32[2,24,4096]{2,1,0:T(8,128)S(1)} %copy-done.3, f32[2,24,4096]{2,1,0:T(8,128)} %collective-permute-done.5.back_ref, f32[4,24,4096]{2,1,0:T(8,128)S(1)} %copy-done, ...), custom_call_target="tpu_custom_call" | custom-call | flops 905969664 | bytes 3932160 | tf_op jit(solution)/shard_map/pallas_call | solution.py:328
  49.0 0.0 collective-permute-done.2.fore_ref
  49.0 0.0 collective-permute-done.3.back_ref
  49.0 3.2 %shard_map.87 = (bf16[4,24,4096]{2,1,0:T(8,128)(2,1)}, f32[16,24,128]{2,1,0:T(8,128)S(1)}) custom-call(s32[128]{0:T(128)S(1)} %bitcast.7, s32[1]{0:T(128)} %bitcast.1.me_ref, f32[1,24,4096]{2,1,0:T(8,128)} %collective-permute-done.2.fore_ref, f32[1,24,4096]{2,1,0:T(8,128)} %collective-permute-done.3.back_ref, ...), custom_call_target="tpu_custom_call", output_to_operand_aliasing={{0}: (10, {})} | custom-call | flops 452984832 | bytes 1966080 | tf_op jit(solution)/shard_map/pallas_call | solution.py:328
  52.2 0.0 collective-permute-done.6.refs_3_
  52.2 0.0 collective-permute-done.fore_ref
  52.2 0.0 collective-permute-done.1.back_ref
  52.2 3.1 %shard_map.88 = (bf16[4,24,4096]{2,1,0:T(8,128)(2,1)}, f32[8,48,128]{2,1,0:T(8,128)S(1)}, f32[8,24,128]{2,1,0:T(8,128)S(1)}) custom-call(s32[128]{0:T(128)S(1)} %bitcast.8, s32[1]{0:T(128)} %bitcast.1.me_ref, f32[1,24,4096]{2,1,0:T(8,128)S(1)} %collective-permute-done.fore_ref, ...), custom_call_target="tpu_custom_call", output_to_operand_aliasing={{0}: (10, {})} | custom-call | flops 452984832 | bytes 1966080 | tf_op jit(solution)/shard_map/pallas_call | solution.py:328
  55.3 0.1 collective-permute-start.7
  55.4 1.2 %collective-permute-done.7 = f32[8,24,128]{2,1,0:T(8,128)S(1)} collective-permute-done((f32[8,24,128]{2,1,0:T(8,128)S(1)}, f32[8,24,128]{2,1,0:T(8,128)S(1)}, u32[]{:S(2)}, u32[]{:S(2)}) %collective-permute-start.7) | collective-permute-done | bytes 98336 | tf_op jit(solution)/shard_map/ppermute | solution.py:229
  56.6 2.8 %collective-permute-start.8 = (f32[4,48,128]{2,1,0:T(8,128)S(1)}, f32[4,48,128]{2,1,0:T(8,128)S(1)}, u32[]{:S(2)}, u32[]{:S(2)}) collective-permute-start(f32[4,48,128]{2,1,0:T(8,128)S(1)} %pad_maximum_fusion), channel_id=1, source_target_pairs={{0,2},{1,3},{2,0},{3,1},{4,6},{5,7},{6,4},{7,5},{8,10},{9,11},{10,... | collective-permute-start | bytes 294920 | tf_op jit(solution)/shard_map/ppermute | solution.py:229
  59.5 3.1 %collective-permute-done.8 = f32[4,48,128]{2,1,0:T(8,128)S(1)} collective-permute-done((f32[4,48,128]{2,1,0:T(8,128)S(1)}, f32[4,48,128]{2,1,0:T(8,128)S(1)}, u32[]{:S(2)}, u32[]{:S(2)}) %collective-permute-start.8) | collective-permute-done | bytes 98336 | tf_op jit(solution)/shard_map/ppermute | solution.py:229
  62.6 1.6 %collective-permute-start.9 = (f32[2,48,128]{2,1,0:T(8,128)S(1)}, f32[2,48,128]{2,1,0:T(8,128)S(1)}, u32[]{:S(2)}, u32[]{:S(2)}) collective-permute-start(f32[2,48,128]{2,1,0:T(8,128)S(1)} %slice.55), channel_id=1, source_target_pairs={{0,4},{1,5},{2,6},{3,7},{4,0},{5,1},{6,2},{7,3},{8,12},{9,13},{10,... | collective-permute-start | bytes 147464 | tf_op jit(solution)/shard_map/ppermute | solution.py:229
  64.2 2.5 %collective-permute-done.9 = f32[2,48,128]{2,1,0:T(8,128)S(1)} collective-permute-done((f32[2,48,128]{2,1,0:T(8,128)S(1)}, f32[2,48,128]{2,1,0:T(8,128)S(1)}, u32[]{:S(2)}, u32[]{:S(2)}) %collective-permute-start.9) | collective-permute-done | bytes 49184 | tf_op jit(solution)/shard_map/ppermute | solution.py:229
  66.8 2.7 %collective-permute-start.10 = (f32[1,48,128]{2,1,0:T(8,128)S(1)}, f32[1,48,128]{2,1,0:T(8,128)S(1)}, u32[]{:S(2)}, u32[]{:S(2)}) collective-permute-start(f32[1,48,128]{2,1,0:T(8,128)S(1)} %slice.57), channel_id=1, source_target_pairs={{0,8},{1,9},{2,10},{3,11},{4,12},{5,13},{6,14},{7,15},{8,0},{9,1},... | collective-permute-start | bytes 73736 | tf_op jit(solution)/shard_map/ppermute | solution.py:229
  69.4 2.1 %collective-permute-done.10 = f32[1,48,128]{2,1,0:T(8,128)S(1)} collective-permute-done((f32[1,48,128]{2,1,0:T(8,128)S(1)}, f32[1,48,128]{2,1,0:T(8,128)S(1)}, u32[]{:S(2)}, u32[]{:S(2)}) %collective-permute-start.10) | collective-permute-done | bytes 24608 | tf_op jit(solution)/shard_map/ppermute | solution.py:229
  71.6 0.6 fusion.2
  (7 shorter events, 0.1 us)
Async XLA Ops:
  0.6 6.1 %copy-start = (f32[4,24,4096]{2,1,0:T(8,128)S(1)}, f32[4,24,4096]{2,1,0:T(8,128)}, u32[]{:S(2)}) copy-start(f32[4,24,4096]{2,1,0:T(8,128)} %image_ref.5) | copy-start | bytes 4718596
  0.6 20.0 %copy-start.4 = (s32[128,1]{0,1:T(1,128)S(1)}, s32[128,1]{0,1:T(1,128)}, u32[]{:S(2)}) copy-start(s32[128,1]{0,1:T(1,128)} %param.13) | copy-start | bytes 1540
  0.6 20.0 %copy-start.1 = (f32[4,24,4096]{2,1,0:T(8,128)S(1)}, f32[4,24,4096]{2,1,0:T(8,128)}, u32[]{:S(2)}) copy-start(f32[4,24,4096]{2,1,0:T(8,128)} %inv_ref.7) | copy-start | bytes 4718596
  2.9 18.9 %copy-start.5 = (f32[4,3,41]{2,0,1:T(4,128)S(1)}, f32[4,3,41]{2,0,1:T(4,128)}, u32[]{:S(2)}) copy-start(f32[4,3,41]{2,0,1:T(4,128)} %param.11) | copy-start | bytes 5908
  2.9 18.9 %copy-start.7 = (f32[4,2]{0,1:T(2,128)S(1)}, f32[4,2]{0,1:T(2,128)}, u32[]{:S(2)}) copy-start(f32[4,2]{0,1:T(2,128)} %param.9) | copy-start | bytes 100
  2.9 15.5 %collective-permute-start.4 = (f32[2,24,4096]{2,1,0:T(8,128)}, f32[2,24,4096]{2,1,0:T(8,128)S(1)}, u32[]{:S(2)}, u32[]{:S(2)}) collective-permute-start(f32[2,24,4096]{2,1,0:T(8,128)} %slice.41), channel_id=1, source_target_pairs={{0,1},{1,2},{2,3},{3,4},{4,5},{5,6},{6,7},{7,8},{8,9},{9,10},{10,1... | collective-permute-start | bytes 2359304 | tf_op jit(solution)/shard_map/ppermute | solution.py:257
  5.5 22.5 %collective-permute-start.5 = (f32[2,24,4096]{2,1,0:T(8,128)}, f32[2,24,4096]{2,1,0:T(8,128)}, u32[]{:S(2)}, u32[]{:S(2)}) collective-permute-start(f32[2,24,4096]{2,1,0:T(8,128)} %slice.41), channel_id=1, source_target_pairs={{1,0},{2,1},{3,2},{4,3},{5,4},{6,5},{7,6},{8,7},{9,8},{10,9},{11,1... | collective-permute-start | bytes 2359304 | tf_op jit(solution)/shard_map/ppermute | solution.py:258
  7.7 41.3 %collective-permute-start.2 = (f32[1,24,4096]{2,1,0:T(8,128)}, f32[1,24,4096]{2,1,0:T(8,128)}, u32[]{:S(2)}, u32[]{:S(2)}) collective-permute-start(f32[1,24,4096]{2,1,0:T(8,128)} %get-tuple-element.26), channel_id=1, source_target_pairs={{0,1},{1,2},{2,3},{3,4},{4,5},{5,6},{6,7},{7,8},{8,9},{9,10},{10,1... | collective-permute-start | bytes 1179656 | tf_op jit(solution)/shard_map/ppermute | solution.py:257
  13.5 35.5 %collective-permute-start.3 = (f32[1,24,4096]{2,1,0:T(8,128)}, f32[1,24,4096]{2,1,0:T(8,128)}, u32[]{:S(2)}, u32[]{:S(2)}) collective-permute-start(f32[1,24,4096]{2,1,0:T(8,128)} %get-tuple-element.26), channel_id=1, source_target_pairs={{1,0},{2,1},{3,2},{4,3},{5,4},{6,5},{7,6},{8,7},{9,8},{10,9},{11,1... | collective-permute-start | bytes 1179656 | tf_op jit(solution)/shard_map/ppermute | solution.py:258
  14.8 37.4 %collective-permute-start = (f32[1,24,4096]{2,1,0:T(8,128)}, f32[1,24,4096]{2,1,0:T(8,128)S(1)}, u32[]{:S(2)}, u32[]{:S(2)}) collective-permute-start(f32[1,24,4096]{2,1,0:T(8,128)} %get-tuple-element.27), channel_id=1, source_target_pairs={{0,1},{1,2},{2,3},{3,4},{4,5},{5,6},{6,7},{7,8},{8,9},{9,10},{10,1... | collective-permute-start | bytes 1179656 | tf_op jit(solution)/shard_map/ppermute | solution.py:257
  18.4 0.9 %copy-start.2 = (f32[2,24,4096]{2,1,0:T(8,128)}, f32[2,24,4096]{2,1,0:T(8,128)S(1)}, u32[]{:S(2)}) copy-start(f32[2,24,4096]{2,1,0:T(8,128)S(1)} %collective-permute-done.4.fore_ref) | copy-start | bytes 2359300
  19.4 32.9 %collective-permute-start.1 = (f32[1,24,4096]{2,1,0:T(8,128)}, f32[1,24,4096]{2,1,0:T(8,128)}, u32[]{:S(2)}, u32[]{:S(2)}) collective-permute-start(f32[1,24,4096]{2,1,0:T(8,128)} %get-tuple-element.27), channel_id=1, source_target_pairs={{1,0},{2,1},{3,2},{4,3},{5,4},{6,5},{7,6},{8,7},{9,8},{10,9},{11,1... | collective-permute-start | bytes 1179656 | tf_op jit(solution)/shard_map/ppermute | solution.py:258
  20.7 23.7 %copy-start.3 = (f32[2,24,4096]{2,1,0:T(8,128)S(1)}, f32[2,24,4096]{2,1,0:T(8,128)}, u32[]{:S(2)}) copy-start(f32[2,24,4096]{2,1,0:T(8,128)} %copy-done.2) | copy-start | bytes 2359300
  21.8 0.7 copy-start.6
  22.5 0.7 copy-start.8
  28.0 24.2 %collective-permute-start.6 = (f32[8,24,128]{2,1,0:T(8,128)S(1)}, f32[8,24,128]{2,1,0:T(8,128)S(1)}, u32[]{:S(2)}, u32[]{:S(2)}) collective-permute-start(f32[8,24,128]{2,1,0:T(8,128)S(1)} %get-tuple-element.22), channel_id=1, source_target_pairs={{0,1},{1,0},{2,3},{3,2},{4,5},{5,4},{6,7},{7,6},{8,9},{9,8},{10,11... | collective-permute-start | bytes 294920 | tf_op jit(solution)/shard_map/ppermute | solution.py:229
  55.3 1.3 %collective-permute-start.7 = (f32[8,24,128]{2,1,0:T(8,128)S(1)}, f32[8,24,128]{2,1,0:T(8,128)S(1)}, u32[]{:S(2)}, u32[]{:S(2)}) collective-permute-start(f32[8,24,128]{2,1,0:T(8,128)S(1)} %get-tuple-element.25), channel_id=1, source_target_pairs={{0,1},{1,0},{2,3},{3,2},{4,5},{5,4},{6,7},{7,6},{8,9},{9,8},{10,11... | collective-permute-start | bytes 294920 | tf_op jit(solution)/shard_map/ppermute | solution.py:229
  56.6 5.9 %collective-permute-start.8 = (f32[4,48,128]{2,1,0:T(8,128)S(1)}, f32[4,48,128]{2,1,0:T(8,128)S(1)}, u32[]{:S(2)}, u32[]{:S(2)}) collective-permute-start(f32[4,48,128]{2,1,0:T(8,128)S(1)} %pad_maximum_fusion), channel_id=1, source_target_pairs={{0,2},{1,3},{2,0},{3,1},{4,6},{5,7},{6,4},{7,5},{8,10},{9,11},{10,... | collective-permute-start | bytes 294920 | tf_op jit(solution)/shard_map/ppermute | solution.py:229
  62.6 4.2 %collective-permute-start.9 = (f32[2,48,128]{2,1,0:T(8,128)S(1)}, f32[2,48,128]{2,1,0:T(8,128)S(1)}, u32[]{:S(2)}, u32[]{:S(2)}) collective-permute-start(f32[2,48,128]{2,1,0:T(8,128)S(1)} %slice.55), channel_id=1, source_target_pairs={{0,4},{1,5},{2,6},{3,7},{4,0},{5,1},{6,2},{7,3},{8,12},{9,13},{10,... | collective-permute-start | bytes 147464 | tf_op jit(solution)/shard_map/ppermute | solution.py:229
  66.8 4.8 %collective-permute-start.10 = (f32[1,48,128]{2,1,0:T(8,128)S(1)}, f32[1,48,128]{2,1,0:T(8,128)S(1)}, u32[]{:S(2)}, u32[]{:S(2)}) collective-permute-start(f32[1,48,128]{2,1,0:T(8,128)S(1)} %slice.57), channel_id=1, source_target_pairs={{0,8},{1,9},{2,10},{3,11},{4,12},{5,13},{6,14},{7,15},{8,0},{9,1},... | collective-permute-start | bytes 73736 | tf_op jit(solution)/shard_map/ppermute | solution.py:229

commit v3 on v2

--- a/solution.py
+++ b/solution.py
@@ -14,6 +14,7 @@
 BF16 = jnp.bfloat16
 HIGHEST = lax.Precision.HIGHEST
 GRANT = 24 * 1024 * 1024
+GROUPS = 2
 
 
 def round_up(number, unit):
@@ -65,24 +66,45 @@
     return jnp.concatenate([block, jnp.zeros((rows - high, lanes), F32)], axis=0)
 
 
-def weights_kernel(order, place_ref, me_ref, inv_ref, keep_ref, send_ref, den_ref):
+def pack_kernel(image_ref, fore_ref, back_ref):
+    height, width = image_ref.shape[1:]
+    tail = width // 8
+    body = width - tail
+    sub = row_of((8, tail))
+    for ref, row, spare in ((fore_ref, 0, 0), (back_ref, height - 8, 7)):
+        ends = image_ref[0, row : row + 8, body:]
+        packed = []
+        for j, r in enumerate(r for r in range(8) if r != spare):
+            moved = pltpu.roll(ends, (spare - r) % 8, 0)
+            part = image_ref[0, row : row + 8, j * tail : (j + 1) * tail]
+            packed.append(jnp.where(sub == spare, moved, part))
+        incomplete = [jnp.concatenate(packed, axis=1)]
+        full = [image_ref[0, t : t + 8, :] for t in range(0, height, 8) if t != row]
+        lanes = 0
+        for part in incomplete + full if row == 0 else full + incomplete:
+            ref[0, :, lanes : lanes + part.shape[1]] = part
+            lanes += part.shape[1]
+
+
+def weights_kernel(order, place_ref, inv_ref, keep_ref, send_ref, den_ref):
     visits, _, width = inv_ref.shape
     pieces = width // PC
     den_ref[...] = jnp.zeros_like(den_ref)
     for n in range(visits * pieces):
-        slot = place_ref[n] ^ me_ref[0]
+        slot = place_ref[n]
         span = slice(n % pieces * PC, (n % pieces + 1) * PC)
-        den_ref[slot] += inv_ref[n // pieces, :, span]
+        den_ref[n % 2, slot] += inv_ref[n // pieces, :, span]
     hand_out(order, den_ref, keep_ref, send_ref)
 
 
 def hand_out(order, acc_ref, keep_ref, send_ref):
     half = len(order) // 2
     for i, slot in enumerate(order):
+        total = acc_ref[0, slot] + acc_ref[1, slot]
         if i < half:
-            keep_ref[i, : acc_ref.shape[1]] = acc_ref[slot]
+            keep_ref[i, : acc_ref.shape[2]] = total
         else:
-            send_ref[i - half] = acc_ref[slot]
+            send_ref[i - half] = total
 
 
 def prepare_kernel(
@@ -142,7 +164,7 @@
 
 
 def match_kernel(
-    bases, first, last, order, place_ref, me_ref, fore_ref, back_ref, image_ref, inv_ref, rows_ref, cols_ref,
+    bases, first, last, order, place_ref, fore_ref, back_ref, image_ref, inv_ref, rows_ref, cols_ref,
     edge_ref, *refs
 ):
     if first:
@@ -159,10 +181,34 @@
     pad = round_up(3 * height, 16)
     deep = rows_ref.shape[2]
     operator = rows_ref[visit]
+    tail = width // 8
+    body = width - tail
+    split_at = body // PC
+
+    def unpacked(ref, n, base, spare):
+        if n < split_at:
+            return ref[step, :, base + n * PC : base + (n + 1) * PC]
+        parts = []
+        for r in range(8):
+            j = r - (r > spare)
+            at = base + j * tail + (n - split_at) * PC
+            if r == spare:
+                parts.append(jnp.zeros((1, PC), F32))
+            else:
+                parts.append(ref[step, spare : spare + 1, at : at + PC])
+        return jnp.concatenate(parts, axis=0)
 
     def column(n):
-        span = slice(n * PC, (n + 1) * PC)
-        parts = [fore_ref[step, :, span], image_ref[visit, :, span], back_ref[step, :, span]]
+        full = height // 8 - 1
+        parts = [unpacked(fore_ref, n, 0, 0)]
+        for t in range(full):
+            at = body + t * width + n * PC
+            parts.append(fore_ref[step, :, at : at + PC])
+        parts.append(image_ref[visit, :, n * PC : (n + 1) * PC])
+        for t in range(full):
+            at = t * width + n * PC
+            parts.append(back_ref[step, :, at : at + PC])
+        parts.append(unpacked(back_ref, n, full * width, 7))
         if pad > 3 * height:
             parts.append(jnp.zeros((pad - 3 * height, PC), F32))
         return jnp.concatenate(parts, axis=0)
@@ -174,7 +220,7 @@
             high_ref[k, pair * 2 * height : (pair + 1) * 2 * height, :] = high
             low_ref[k, pair * 2 * height : (pair + 1) * 2 * height, :] = low
 
-    for pair in range(pairs):
+    def fill(pair):
         stacked = jnp.concatenate([column(pair), column(pair + pairs)], axis=1)
         high, low = split(stacked)
         depth = [high, high, low]
@@ -198,25 +244,41 @@
         low = jnp.dot(window(low_ref, start, count), ref[visit, :, :PC], preferred_element_type=F32)
         return high[:, :PC] + high[:, PC:] + low
 
-    main = blocks(0, pairs, cols_ref)
-    edge = blocks(pairs - 1, 1, edge_ref)[height:]
-    turned = [None] * pieces
-    for n in range(pieces):
-        row = (2 * (n % pairs) + n // pairs) * height
-        block = main[row : row + height] if n < pieces - 1 else edge
-        turned[n] = pltpu.roll(block, PC // 2, 1)
-    lane = lane_of((height, PC))
-
     @pl.when(step == 0)
     def _():
         acc_ref[...] = old_ref[...] if first else jnp.zeros_like(acc_ref)
 
-    for c in range(pieces):
-        piece = jnp.where(lane < PC // 2, turned[c - 1], turned[c])
-        span = slice(c * PC, (c + 1) * PC)
-        out_ref[0, :, span] = piece.astype(BF16)
-        slot = place_ref[visit * pieces + c] ^ me_ref[0]
-        acc_ref[slot] += inv_ref[visit, :, span] * piece
+    lane = lane_of((height, PC))
+    turned = {}
+    done = set()
+
+    def finish():
+        for c in range(pieces):
+            if c in done or c not in turned or (c - 1) % pieces not in turned:
+                continue
+            done.add(c)
+            piece = jnp.where(lane < PC // 2, turned[(c - 1) % pieces], turned[c])
+            span = slice(c * PC, (c + 1) * PC)
+            out_ref[0, :, span] = piece.astype(BF16)
+            slot = place_ref[visit * pieces + c]
+            acc_ref[c % 2, slot] += inv_ref[visit, :, span] * piece
+
+    for pair in range(min(pairs, pairs // GROUPS + 1)):
+        fill(pair)
+    for group in range(GROUPS):
+        start, count = group * pairs // GROUPS, pairs // GROUPS
+        main = blocks(start, count, cols_ref)
+        for pair in range(start + count + 1, min(pairs, start + 2 * count + 1)):
+            fill(pair)
+        if group == GROUPS - 1:
+            edge = blocks(pairs - 1, 1, edge_ref)[height:]
+        for pair in range(start, start + count):
+            for h in (0, 1):
+                n = pair + h * pairs
+                row = (2 * (pair - start) + h) * height
+                block = main[row : row + height] if n < pieces - 1 else edge
+                turned[n] = pltpu.roll(block, PC // 2, 1)
+        finish()
 
     if last:
         @pl.when(step == pl.num_programs(0) - 1)
@@ -234,10 +296,11 @@
     bases, length = psf_rows.shape[1:]
     size = lax.axis_size("tile")
     reach = length // 2 + TAPS
-    if size & (size - 1) or reach > height or height % 8 or width % WIDE or visits < 3:
+    if size & (size - 1) or reach != height - 1 or height % 8 or width % (8 * PC) or visits < 3:
         raise ValueError("unsupported sizes")
-    me = lax.axis_index("tile").astype(jnp.int32).reshape(1)
-    place = placement.reshape(-1)
+    index = lax.axis_index("tile").astype(jnp.int32)
+    place = placement.reshape(-1) ^ index
+    me = index.reshape(1)
     bits = [1 << b for b in range(size.bit_length() - 1)]
     order = [0]
     for bit in reversed(bits):
@@ -249,27 +312,36 @@
     vmem = pl.BlockSpec(memory_space=pltpu.VMEM)
     anywhere = pl.BlockSpec(memory_space=pl.ANY)
     params = pltpu.CompilerParams(vmem_limit_bytes=GRANT)
+    lanes = height * width // 8 - width // 8
     chunks = ((0, visits - 2), (visits - 2, 1), (visits - 1, 1))
 
     halos = []
     for (first, count) in chunks:
-        part = image[first : first + count]
-        fore = lax.ppermute(part, "tile", rising)
-        back = lax.ppermute(part, "tile", falling)
+        block = pl.BlockSpec((1, 8, lanes), lambda v: (v, 0, 0))
+        fore, back = pl.pallas_call(
+            pack_kernel,
+            grid=(count,),
+            in_specs=[pl.BlockSpec((1, height, width), lambda v, first=first: (v + first, 0, 0))],
+            out_specs=[block] * 2,
+            out_shape=[jax.ShapeDtypeStruct((count, 8, lanes), F32)] * 2,
+            compiler_params=pltpu.CompilerParams(vmem_limit_bytes=60 * 1024 * 1024),
+        )(image)
+        fore = lax.ppermute(fore, "tile", rising)
+        back = lax.ppermute(back, "tile", falling)
         halos.append((fore, back))
 
     half = jax.ShapeDtypeStruct((size // 2, height, PC), F32)
-    sums = pltpu.VMEM((size, height, PC), F32)
+    sums = pltpu.VMEM((2, size, height, PC), F32)
     weights = pl.pallas_call(
         functools.partial(weights_kernel, order),
-        in_specs=[smem, smem, vmem],
+        in_specs=[smem, vmem],
         out_specs=[vmem, vmem],
         out_shape=[half, half],
         scratch_shapes=[sums],
         compiler_params=params,
         name="weights",
     )
-    den = weights(place, me, inv_var)
+    den = weights(place, inv_var)
     denom = (den[0], exchange(den[1], size, bits[0]))
 
     deep = round_up(3 * round_up(3 * height, 16), 128)
@@ -308,16 +380,16 @@
             specs += [vmem, vmem]
             scratch += [sums]
         else:
-            shapes += [jax.ShapeDtypeStruct((size, height, PC), F32)]
+            shapes += [jax.ShapeDtypeStruct((2, size, height, PC), F32)]
             specs += [vmem]
         match = pl.pallas_call(
             functools.partial(match_kernel, bases, first, last, order),
             grid=(count,),
-            in_specs=[smem, smem] + inputs,
+            in_specs=[smem] + inputs,
             out_specs=specs,
             out_shape=shapes,
             scratch_shapes=scratch,
-            input_output_aliases={10: 0} if first else {},
+            input_output_aliases={9: 0} if first else {},
             compiler_params=params,
             cost_estimate=pl.CostEstimate(
                 flops=count * 6 * bases * height * width * WIDE,
@@ -325,13 +397,20 @@
                 transcendentals=0,
             ),
         )
-        carried = match(place, me, fore, back, image, inv_var, *operators, *extra)
+        carried = match(place, fore, back, image, inv_var, *operators, *extra)
     matched, keep, send = carried
     received = exchange(send, size, bits[0])
     keep = jnp.concatenate([keep[:, :height] + received, keep[:, height:]], axis=1)
-    for bit in bits[1:]:
-        count = keep.shape[0] // 2
-        keep = keep[:count] + exchange(keep[count:], size, bit)
+    rest = bits[1:]
+    while rest:
+        near, rest = rest[:2], rest[2:]
+        masks = [0, near[1], near[0], sum(near)] if len(near) > 1 else [0, near[0]]
+        count = keep.shape[0] // len(masks)
+        parts = {mask: keep[i * count : (i + 1) * count] for i, mask in enumerate(masks)}
+        total = parts[0]
+        for mask in sorted(parts, reverse=True)[:-1]:
+            total = total + exchange(parts[mask], size, mask)
+        keep = total
     return matched, keep[:, :height] / jnp.maximum(keep[:, height:], 1.0)
 
 

time: 72.6 us -> 63.4 us (0.87)
  starting transfers between devices: 39.4 us -> 31 us
  Pallas kernels: 16.8 us -> 23 us
  local copies, waits for them, and re-layouts: 5.47 us -> 0.03 us
  waiting for transfers between devices: 9.01 us -> 7.47 us
    ppermute x5 -> x6, starting transfers between devices: 23.6 us -> 15 us  [exchange(): return lax.ppermute(send, 'tile', [(i, i ^ bit) for i in range(size)])]
    pallas_call x4 -> x7, Pallas kernels: 12 us -> 18.2 us  [the longest x3 11.2 us: on_device(): carried = match(place, fore, back, image, inv_var, *operators, *extra)]
    slice x4 -> x1, local copies, waits for them, and re-layouts: 3.17 us -> 0.01 us  [on_device(): keep[i * count:(i + 1) * count]]
    unnamed x18 -> x14, local copies, waits for them, and re-layouts: 2.3 us -> 0.03 us
    ppermute x5 -> x6, waiting for transfers between devices: 9 us -> 7.45 us  [exchange(): return lax.ppermute(send, 'tile', [(i, i ^ bit) for i in range(size)])]
  transfers between devices with their start and end apart: 11 -> 12, of which waited for: 4 -> 4; matrix products, arithmetic and copies ran while one was open for 1% -> 0% of each run, Pallas kernels for 19% -> 28%
where the time goes in v3:
time: 63.4 us; the launch traced here: 62.9 us
  starting transfers between devices  31 us (49%)
  Pallas kernels  23 us (36%)
  waiting for transfers between devices  7.47 us (12%)
  between operations  0.8 us (1%)
  other arithmetic  0.66 us (1%)
    ppermute x6, starting transfers between devices, exchange(): return lax.ppermute(send, 'tile', [(i, i ^ bit) for i in range(size)])  15 us
    ppermute x3, starting transfers between devices, on_device(): fore = lax.ppermute(fore, 'tile', rising)  11.9 us
    pallas_call x3, Pallas kernels, on_device(): carried = match(place, fore, back, image, inv_var, *operators, *extra)  11.2 us
    ppermute x6, waiting for transfers between devices, exchange(): return lax.ppermute(send, 'tile', [(i, i ^ bit) for i in range(size)])  7.45 us
    pallas_call x3, Pallas kernels, on_device(): pl.pallas_call(pack_kernel, grid=(count,), in_specs=[pl.BlockSpec((1, hei...  5.97 us
    pallas_call x1, Pallas kernels, on_device(): prepare(me, shift.T, col_offset, psf_rows.transpose(1, 0, 2), psf_cols.tr...  4.78 us
    ppermute x3, starting transfers between devices, on_device(): back = lax.ppermute(back, 'tile', falling)  4.13 us
  transfers between devices with their start and end apart: 12, of which 4 were waited for; matrix products, arithmetic and copies ran while one was open for 0% of the time, Pallas kernels for 28%

profile of v3, /device:TPU:0, one launch (start us, length us, event | category | flops | bytes accessed | tf_op | source)
XLA Modules:
  0.0 62.9 jit_solution(15212973017521407637)
XLA Ops:
  0.6 2.2 %shard_map.88 = (f32[2,8,11776]{2,1,0:T(8,128)}, f32[2,8,11776]{2,1,0:T(8,128)}) custom-call(f32[4,24,4096]{2,1,0:T(8,128)} %image_ref.11), custom_call_target="tpu_custom_call" | custom-call | tf_op jit(solution)/shard_map/pallas_call | solution.py:321
  2.8 3.3 %collective-permute-start.4 = (f32[2,8,11776]{2,1,0:T(8,128)}, f32[2,8,11776]{2,1,0:T(8,128)}, u32[]{:S(2)}, u32[]{:S(2)}) collective-permute-start(f32[2,8,11776]{2,1,0:T(8,128)} %get-tuple-element.27), channel_id=1, source_target_pairs={{0,1},{1,2},{2,3},{3,4},{4,5},{5,6},{6,7},{7,8},{8,9},{9,10},{10,1... | collective-permute-start | bytes 2261000 | tf_op jit(solution)/shard_map/ppermute | solution.py:329
  6.1 0.0 copy-start.6
  6.1 0.0 copy-start.1
  6.1 1.4 %collective-permute-start.5 = (f32[2,8,11776]{2,1,0:T(8,128)}, f32[2,8,11776]{2,1,0:T(8,128)}, u32[]{:S(2)}, u32[]{:S(2)}) collective-permute-start(f32[2,8,11776]{2,1,0:T(8,128)} %get-tuple-element.28), channel_id=1, source_target_pairs={{1,0},{2,1},{3,2},{4,3},{5,4},{6,5},{7,6},{8,7},{9,8},{10,9},{11,1... | collective-permute-start | bytes 2261000 | tf_op jit(solution)/shard_map/ppermute | solution.py:330
  7.5 1.9 %shard_map.87 = (f32[1,8,11776]{2,1,0:T(8,128)}, f32[1,8,11776]{2,1,0:T(8,128)}) custom-call(f32[4,24,4096]{2,1,0:T(8,128)} %image_ref.11), custom_call_target="tpu_custom_call" | custom-call | tf_op jit(solution)/shard_map/pallas_call | solution.py:321
  9.4 5.0 %collective-permute-start.2 = (f32[1,8,11776]{2,1,0:T(8,128)}, f32[1,8,11776]{2,1,0:T(8,128)}, u32[]{:S(2)}, u32[]{:S(2)}) collective-permute-start(f32[1,8,11776]{2,1,0:T(8,128)} %get-tuple-element.25), channel_id=1, source_target_pairs={{0,1},{1,2},{2,3},{3,4},{4,5},{5,6},{6,7},{7,8},{8,9},{9,10},{10,1... | collective-permute-start | bytes 1130504 | tf_op jit(solution)/shard_map/ppermute | solution.py:329
  14.4 0.0 copy-start.2
  14.4 0.0 copy-start.3
  14.4 0.0 copy-start.4
  14.4 0.0 copy-start.5
  14.4 0.0 copy-start
  14.5 1.4 %collective-permute-start.3 = (f32[1,8,11776]{2,1,0:T(8,128)}, f32[1,8,11776]{2,1,0:T(8,128)}, u32[]{:S(2)}, u32[]{:S(2)}) collective-permute-start(f32[1,8,11776]{2,1,0:T(8,128)} %get-tuple-element.26), channel_id=1, source_target_pairs={{1,0},{2,1},{3,2},{4,3},{5,4},{6,5},{7,6},{8,7},{9,8},{10,9},{11,1... | collective-permute-start | bytes 1130504 | tf_op jit(solution)/shard_map/ppermute | solution.py:330
  15.9 1.9 %shard_map.86 = (f32[1,8,11776]{2,1,0:T(8,128)}, f32[1,8,11776]{2,1,0:T(8,128)}) custom-call(f32[4,24,4096]{2,1,0:T(8,128)} %image_ref.11), custom_call_target="tpu_custom_call" | custom-call | tf_op jit(solution)/shard_map/pallas_call | solution.py:321
  17.8 3.6 %collective-permute-start = (f32[1,8,11776]{2,1,0:T(8,128)}, f32[1,8,11776]{2,1,0:T(8,128)S(1)}, u32[]{:S(2)}, u32[]{:S(2)}) collective-permute-start(f32[1,8,11776]{2,1,0:T(8,128)} %get-tuple-element.20), channel_id=1, source_target_pairs={{0,1},{1,2},{2,3},{3,4},{4,5},{5,6},{6,7},{7,8},{8,9},{9,10},{10,1... | collective-permute-start | bytes 1130504 | tf_op jit(solution)/shard_map/ppermute | solution.py:329
  21.4 0.0 collective-permute-done.4.fore_ref
  21.4 1.3 %collective-permute-start.1 = (f32[1,8,11776]{2,1,0:T(8,128)}, f32[1,8,11776]{2,1,0:T(8,128)}, u32[]{:S(2)}, u32[]{:S(2)}) collective-permute-start(f32[1,8,11776]{2,1,0:T(8,128)} %get-tuple-element.21), channel_id=1, source_target_pairs={{1,0},{2,1},{3,2},{4,3},{5,4},{6,5},{7,6},{8,7},{9,8},{10,9},{11,1... | collective-permute-start | bytes 1130504 | tf_op jit(solution)/shard_map/ppermute | solution.py:330
  22.7 0.0 copy-done.6
  22.7 0.0 copy-done.1
  22.7 1.1 %weights.1 = (f32[8,24,128]{2,1,0:T(8,128)S(1)}, f32[8,24,128]{2,1,0:T(8,128)S(1)}) custom-call(s32[128]{0:T(128)S(1)} %xor_bitcast_fusion.place_ref, f32[4,24,4096]{2,1,0:T(8,128)S(1)} %copy-done.1), custom_call_target="tpu_custom_call" | custom-call | tf_op jit(solution)/shard_map/weights/pallas_call | solution.py:344
  23.8 0.0 copy-done.2
  23.8 0.0 copy-done.3
  23.8 0.0 copy-done.4
  23.8 0.0 copy-done.5
  23.8 4.8 %prepare.1 = (bf16[4,72,256]{2,1,0:T(8,128)(2,1)S(1)}, bf16[4,768,256]{2,1,0:T(8,128)(2,1)S(1)}, bf16[4,768,256]{2,1,0:T(8,128)(2,1)S(1)}) custom-call(s32[1]{0:T(128)} %bitcast.1.me_ref, f32[2,4]{1,0:T(2,128)S(1)} %bitcast.8, s32[4]{0:T(128)S(1)} %copy-done.5, f32[3,4,41]{2,1,0:T(4,128)S(1)} %bitcast.6, f32[3,4,41]{2,1,0:T(4,128)S(1)} %bitcast.7), custom_call_target="tpu_custom_call" | custom-call | tf_op jit(solution)/shard_map/prepare/pallas_call | solution.py:360
  28.6 0.0 collective-permute-done.5.back_ref
  28.6 8.1 %collective-permute-start.6 = (f32[8,24,128]{2,1,0:T(8,128)S(1)}, f32[8,24,128]{2,1,0:T(8,128)S(1)}, u32[]{:S(2)}, u32[]{:S(2)}) collective-permute-start(f32[8,24,128]{2,1,0:T(8,128)S(1)} %get-tuple-element.34), channel_id=1, source_target_pairs={{0,1},{1,0},{2,3},{3,2},{4,5},{5,4},{6,7},{7,6},{8,9},{9,8},{10,11... | collective-permute-start | bytes 294920 | tf_op jit(solution)/shard_map/ppermute | solution.py:291
  36.7 0.0 copy-done
  36.7 4.9 %shard_map.89 = (bf16[4,24,4096]{2,1,0:T(8,128)(2,1)}, f32[2,16,24,128]{3,2,1,0:T(8,128)S(1)}) custom-call(s32[128]{0:T(128)S(1)} %xor_bitcast_fusion.place_ref, f32[2,8,11776]{2,1,0:T(8,128)} %collective-permute-done.4.fore_ref, f32[2,8,11776]{2,1,0:T(8,128)} %collective-permute-done.5.back_ref, f32[4,24,4096]{2,1,0:T(8,128)S(1)} %copy-done, ...), custom_call_target="tpu_custom_call" | custom-call | flops 905969664 | bytes 3932160 | tf_op jit(solution)/shard_map/pallas_call | solution.py:400
  41.6 0.0 collective-permute-done.2.fore_ref
  41.6 0.0 collective-permute-done.3.back_ref
  41.6 3.2 %shard_map.90 = (bf16[4,24,4096]{2,1,0:T(8,128)(2,1)}, f32[2,16,24,128]{3,2,1,0:T(8,128)S(1)}) custom-call(s32[128]{0:T(128)S(1)} %xor_bitcast_fusion.place_ref, f32[1,8,11776]{2,1,0:T(8,128)} %collective-permute-done.2.fore_ref, f32[1,8,11776]{2,1,0:T(8,128)} %collective-permute-done.3.back_ref, ...), custom_call_target="tpu_custom_call", output_to_operand_aliasing={{0}: (9, {})} | custom-call | flops 452984832 | bytes 1966080 | tf_op jit(solution)/shard_map/pallas_call | solution.py:400
  44.8 0.0 collective-permute-done.6.refs_3_
  44.8 0.0 collective-permute-done.fore_ref
  44.8 0.0 collective-permute-done.1.back_ref
  44.8 3.1 %shard_map.91 = (bf16[4,24,4096]{2,1,0:T(8,128)(2,1)}, f32[8,48,128]{2,1,0:T(8,128)S(1)}, f32[8,24,128]{2,1,0:T(8,128)S(1)}) custom-call(s32[128]{0:T(128)S(1)} %xor_bitcast_fusion.place_ref, f32[1,8,11776]{2,1,0:T(8,128)S(1)} %collective-permute-done.fore_ref, f32[1,8,11776]{2,1,0:T(8,128)} %collective-permute-done.1.back_ref, ...), custom_call_target="tpu_custom_call", output_to_operand_aliasing={{0}: (9, {})} | custom-call | flops 452984832 | bytes 1966080 | tf_op jit(solution)/shard_map/pallas_call | solution.py:400
  47.9 0.1 collective-permute-start.7
  48.0 1.2 %collective-permute-done.7 = f32[8,24,128]{2,1,0:T(8,128)S(1)} collective-permute-done((f32[8,24,128]{2,1,0:T(8,128)S(1)}, f32[8,24,128]{2,1,0:T(8,128)S(1)}, u32[]{:S(2)}, u32[]{:S(2)}) %collective-permute-start.7) | collective-permute-done | bytes 98336 | tf_op jit(solution)/shard_map/ppermute | solution.py:291
  49.3 2.9 %collective-permute-start.10 = (f32[2,48,128]{2,1,0:T(8,128)S(1)}, f32[2,48,128]{2,1,0:T(8,128)S(1)}, u32[]{:S(2)}, u32[]{:S(2)}) collective-permute-start(f32[2,48,128]{2,1,0:T(8,128)S(1)} %get-tuple-element.39), channel_id=1, source_target_pairs={{0,2},{1,3},{2,0},{3,1},{4,6},{5,7},{6,4},{7,5},{8,10},{9,11},{10,... | collective-permute-start | bytes 147464 | tf_op jit(solution)/shard_map/ppermute | solution.py:291
  52.2 1.1 %collective-permute-start.8 = (f32[2,48,128]{2,1,0:T(8,128)S(1)}, f32[2,48,128]{2,1,0:T(8,128)S(1)}, u32[]{:S(2)}, u32[]{:S(2)}) collective-permute-start(f32[2,48,128]{2,1,0:T(8,128)S(1)} %get-tuple-element.38), channel_id=1, source_target_pairs={{0,6},{1,7},{2,4},{3,5},{4,2},{5,3},{6,0},{7,1},{8,14},{9,15},{10,... | collective-permute-start | bytes 147464 | tf_op jit(solution)/shard_map/ppermute | solution.py:291
  53.3 0.5 collective-permute-start.9
  53.8 0.6 collective-permute-done.10
  54.4 3.1 %collective-permute-done.8 = f32[2,48,128]{2,1,0:T(8,128)S(1)} collective-permute-done((f32[2,48,128]{2,1,0:T(8,128)S(1)}, f32[2,48,128]{2,1,0:T(8,128)S(1)}, u32[]{:S(2)}, u32[]{:S(2)}) %collective-permute-start.8) | collective-permute-done | bytes 49184 | tf_op jit(solution)/shard_map/ppermute | solution.py:291
  57.5 0.0 collective-permute-done.9
  57.5 2.3 %collective-permute-start.11 = (f32[1,48,128]{2,1,0:T(8,128)S(1)}, f32[1,48,128]{2,1,0:T(8,128)S(1)}, u32[]{:S(2)}, u32[]{:S(2)}) collective-permute-start(f32[1,48,128]{2,1,0:T(8,128)S(1)} %slice.47), channel_id=1, source_target_pairs={{0,8},{1,9},{2,10},{3,11},{4,12},{5,13},{6,14},{7,15},{8,0},{9,1},... | collective-permute-start | bytes 73736 | tf_op jit(solution)/shard_map/ppermute | solution.py:291
  59.9 2.5 %collective-permute-done.11 = f32[1,48,128]{2,1,0:T(8,128)S(1)} collective-permute-done((f32[1,48,128]{2,1,0:T(8,128)S(1)}, f32[1,48,128]{2,1,0:T(8,128)S(1)}, u32[]{:S(2)}, u32[]{:S(2)}) %collective-permute-start.11) | collective-permute-done | bytes 24608 | tf_op jit(solution)/shard_map/ppermute | solution.py:291
  62.3 0.6 fusion.6
  (6 shorter events, 0.1 us)
Async XLA Ops:
  2.8 18.6 %collective-permute-start.4 = (f32[2,8,11776]{2,1,0:T(8,128)}, f32[2,8,11776]{2,1,0:T(8,128)}, u32[]{:S(2)}, u32[]{:S(2)}) collective-permute-start(f32[2,8,11776]{2,1,0:T(8,128)} %get-tuple-element.27), channel_id=1, source_target_pairs={{0,1},{1,2},{2,3},{3,4},{4,5},{5,6},{6,7},{7,8},{8,9},{9,10},{10,1... | collective-permute-start | bytes 2261000 | tf_op jit(solution)/shard_map/ppermute | solution.py:329
  6.1 16.6 %copy-start.6 = (s32[128,1]{0,1:T(1,128)S(1)}, s32[128,1]{0,1:T(1,128)}, u32[]{:S(2)}) copy-start(s32[128,1]{0,1:T(1,128)} %param.13) | copy-start | bytes 1540
  6.1 16.6 %copy-start.1 = (f32[4,24,4096]{2,1,0:T(8,128)S(1)}, f32[4,24,4096]{2,1,0:T(8,128)}, u32[]{:S(2)}) copy-start(f32[4,24,4096]{2,1,0:T(8,128)} %inv_ref.7) | copy-start | bytes 4718596
  6.1 22.5 %collective-permute-start.5 = (f32[2,8,11776]{2,1,0:T(8,128)}, f32[2,8,11776]{2,1,0:T(8,128)}, u32[]{:S(2)}, u32[]{:S(2)}) collective-permute-start(f32[2,8,11776]{2,1,0:T(8,128)} %get-tuple-element.28), channel_id=1, source_target_pairs={{1,0},{2,1},{3,2},{4,3},{5,4},{6,5},{7,6},{8,7},{9,8},{10,9},{11,1... | collective-permute-start | bytes 2261000 | tf_op jit(solution)/shard_map/ppermute | solution.py:330
  9.4 32.2 %collective-permute-start.2 = (f32[1,8,11776]{2,1,0:T(8,128)}, f32[1,8,11776]{2,1,0:T(8,128)}, u32[]{:S(2)}, u32[]{:S(2)}) collective-permute-start(f32[1,8,11776]{2,1,0:T(8,128)} %get-tuple-element.25), channel_id=1, source_target_pairs={{0,1},{1,2},{2,3},{3,4},{4,5},{5,6},{6,7},{7,8},{8,9},{9,10},{10,1... | collective-permute-start | bytes 1130504 | tf_op jit(solution)/shard_map/ppermute | solution.py:329
  14.4 9.4 %copy-start.2 = (f32[4,3,41]{2,0,1:T(4,128)S(1)}, f32[4,3,41]{2,0,1:T(4,128)}, u32[]{:S(2)}) copy-start(f32[4,3,41]{2,0,1:T(4,128)} %param.11) | copy-start | bytes 5908
  14.4 9.4 %copy-start.3 = (f32[4,3,41]{2,0,1:T(4,128)S(1)}, f32[4,3,41]{2,0,1:T(4,128)}, u32[]{:S(2)}) copy-start(f32[4,3,41]{2,0,1:T(4,128)} %param.12) | copy-start | bytes 5908
  14.4 9.4 %copy-start.4 = (f32[4,2]{0,1:T(2,128)S(1)}, f32[4,2]{0,1:T(2,128)}, u32[]{:S(2)}) copy-start(f32[4,2]{0,1:T(2,128)} %param.9) | copy-start | bytes 100
  14.4 9.4 %copy-start.5 = (s32[4]{0:T(128)S(1)}, s32[4]{0:T(128)}, u32[]{:S(2)}) copy-start(s32[4]{0:T(128)} %offset_ref.1) | copy-start | bytes 52
  14.4 22.3 %copy-start = (f32[4,24,4096]{2,1,0:T(8,128)S(1)}, f32[4,24,4096]{2,1,0:T(8,128)}, u32[]{:S(2)}) copy-start(f32[4,24,4096]{2,1,0:T(8,128)} %image_ref.11) | copy-start | bytes 4718596
  14.5 27.2 %collective-permute-start.3 = (f32[1,8,11776]{2,1,0:T(8,128)}, f32[1,8,11776]{2,1,0:T(8,128)}, u32[]{:S(2)}, u32[]{:S(2)}) collective-permute-start(f32[1,8,11776]{2,1,0:T(8,128)} %get-tuple-element.26), channel_id=1, source_target_pairs={{1,0},{2,1},{3,2},{4,3},{5,4},{6,5},{7,6},{8,7},{9,8},{10,9},{11,1... | collective-permute-start | bytes 1130504 | tf_op jit(solution)/shard_map/ppermute | solution.py:330
  17.8 27.0 %collective-permute-start = (f32[1,8,11776]{2,1,0:T(8,128)}, f32[1,8,11776]{2,1,0:T(8,128)S(1)}, u32[]{:S(2)}, u32[]{:S(2)}) collective-permute-start(f32[1,8,11776]{2,1,0:T(8,128)} %get-tuple-element.20), channel_id=1, source_target_pairs={{0,1},{1,2},{2,3},{3,4},{4,5},{5,6},{6,7},{7,8},{8,9},{9,10},{10,1... | collective-permute-start | bytes 1130504 | tf_op jit(solution)/shard_map/ppermute | solution.py:329
  21.4 23.4 %collective-permute-start.1 = (f32[1,8,11776]{2,1,0:T(8,128)}, f32[1,8,11776]{2,1,0:T(8,128)}, u32[]{:S(2)}, u32[]{:S(2)}) collective-permute-start(f32[1,8,11776]{2,1,0:T(8,128)} %get-tuple-element.21), channel_id=1, source_target_pairs={{1,0},{2,1},{3,2},{4,3},{5,4},{6,5},{7,6},{8,7},{9,8},{10,9},{11,1... | collective-permute-start | bytes 1130504 | tf_op jit(solution)/shard_map/ppermute | solution.py:330
  28.6 16.2 %collective-permute-start.6 = (f32[8,24,128]{2,1,0:T(8,128)S(1)}, f32[8,24,128]{2,1,0:T(8,128)S(1)}, u32[]{:S(2)}, u32[]{:S(2)}) collective-permute-start(f32[8,24,128]{2,1,0:T(8,128)S(1)} %get-tuple-element.34), channel_id=1, source_target_pairs={{0,1},{1,0},{2,3},{3,2},{4,5},{5,4},{6,7},{7,6},{8,9},{9,8},{10,11... | collective-permute-start | bytes 294920 | tf_op jit(solution)/shard_map/ppermute | solution.py:291
  47.9 1.3 %collective-permute-start.7 = (f32[8,24,128]{2,1,0:T(8,128)S(1)}, f32[8,24,128]{2,1,0:T(8,128)S(1)}, u32[]{:S(2)}, u32[]{:S(2)}) collective-permute-start(f32[8,24,128]{2,1,0:T(8,128)S(1)} %get-tuple-element.37), channel_id=1, source_target_pairs={{0,1},{1,0},{2,3},{3,2},{4,5},{5,4},{6,7},{7,6},{8,9},{9,8},{10,11... | collective-permute-start | bytes 294920 | tf_op jit(solution)/shard_map/ppermute | solution.py:291
  49.3 5.1 %collective-permute-start.10 = (f32[2,48,128]{2,1,0:T(8,128)S(1)}, f32[2,48,128]{2,1,0:T(8,128)S(1)}, u32[]{:S(2)}, u32[]{:S(2)}) collective-permute-start(f32[2,48,128]{2,1,0:T(8,128)S(1)} %get-tuple-element.39), channel_id=1, source_target_pairs={{0,2},{1,3},{2,0},{3,1},{4,6},{5,7},{6,4},{7,5},{8,10},{9,11},{10,... | collective-permute-start | bytes 147464 | tf_op jit(solution)/shard_map/ppermute | solution.py:291
  52.2 5.3 %collective-permute-start.8 = (f32[2,48,128]{2,1,0:T(8,128)S(1)}, f32[2,48,128]{2,1,0:T(8,128)S(1)}, u32[]{:S(2)}, u32[]{:S(2)}) collective-permute-start(f32[2,48,128]{2,1,0:T(8,128)S(1)} %get-tuple-element.38), channel_id=1, source_target_pairs={{0,6},{1,7},{2,4},{3,5},{4,2},{5,3},{6,0},{7,1},{8,14},{9,15},{10,... | collective-permute-start | bytes 147464 | tf_op jit(solution)/shard_map/ppermute | solution.py:291
  53.3 4.2 %collective-permute-start.9 = (f32[2,48,128]{2,1,0:T(8,128)S(1)}, f32[2,48,128]{2,1,0:T(8,128)S(1)}, u32[]{:S(2)}, u32[]{:S(2)}) collective-permute-start(f32[2,48,128]{2,1,0:T(8,128)S(1)} %get-tuple-element.40), channel_id=1, source_target_pairs={{0,4},{1,5},{2,6},{3,7},{4,0},{5,1},{6,2},{7,3},{8,12},{9,13},{10,... | collective-permute-start | bytes 147464 | tf_op jit(solution)/shard_map/ppermute | solution.py:291
  57.5 4.8 %collective-permute-start.11 = (f32[1,48,128]{2,1,0:T(8,128)S(1)}, f32[1,48,128]{2,1,0:T(8,128)S(1)}, u32[]{:S(2)}, u32[]{:S(2)}) collective-permute-start(f32[1,48,128]{2,1,0:T(8,128)S(1)} %slice.47), channel_id=1, source_target_pairs={{0,8},{1,9},{2,10},{3,11},{4,12},{5,13},{6,14},{7,15},{8,0},{9,1},... | collective-permute-start | bytes 73736 | tf_op jit(solution)/shard_map/ppermute | solution.py:291

commit v4 on v3

--- a/solution.py
+++ b/solution.py
@@ -66,24 +66,31 @@
     return jnp.concatenate([block, jnp.zeros((rows - high, lanes), F32)], axis=0)
 
 
-def pack_kernel(image_ref, fore_ref, back_ref):
+def pack_kernel(me_ref, image_ref, far_ref, near_ref):
     height, width = image_ref.shape[1:]
     tail = width // 8
     body = width - tail
     sub = row_of((8, tail))
-    for ref, row, spare in ((fore_ref, 0, 0), (back_ref, height - 8, 7)):
-        ends = image_ref[0, row : row + 8, body:]
+    tiles = [image_ref[0, t : t + 8, :] for t in range(0, height, 8)]
+
+    def fill(ref, incomplete, full):
+        ends = incomplete[:, body:]
         packed = []
-        for j, r in enumerate(r for r in range(8) if r != spare):
-            moved = pltpu.roll(ends, (spare - r) % 8, 0)
-            part = image_ref[0, row : row + 8, j * tail : (j + 1) * tail]
-            packed.append(jnp.where(sub == spare, moved, part))
-        incomplete = [jnp.concatenate(packed, axis=1)]
-        full = [image_ref[0, t : t + 8, :] for t in range(0, height, 8) if t != row]
+        for r in range(1, 8):
+            part = incomplete[:, (r - 1) * tail : r * tail]
+            packed.append(jnp.where(sub == 0, pltpu.roll(ends, 8 - r, 0), part))
         lanes = 0
-        for part in incomplete + full if row == 0 else full + incomplete:
+        for part in [jnp.concatenate(packed, axis=1)] + full:
             ref[0, :, lanes : lanes + part.shape[1]] = part
             lanes += part.shape[1]
+
+    def both(after_ref, before_ref):
+        fill(after_ref, tiles[0], tiles[1:])
+        fill(before_ref, pltpu.roll(tiles[-1], 1, 0), tiles[:-1])
+
+    odd = lax.rem(me_ref[0], 2)
+    pl.when(odd == 1)(lambda: both(far_ref, near_ref))
+    pl.when(odd == 0)(lambda: both(near_ref, far_ref))
 
 
 def weights_kernel(order, place_ref, inv_ref, keep_ref, send_ref, den_ref):
@@ -127,7 +134,19 @@
             one = jnp.where(lane < height, band(kernels[k : k + 1], PC - (height + half)), 0.0)
             psf = psf + (pltpu.roll(one, k * height, 1) if k else one)
         rows = jnp.dot(warp, psf, precision=HIGHEST, preferred_element_type=F32)
-        rows = jnp.where(row < ext, rows, 0.0).T[: bases * height]
+        above = rows[:height]
+        below = [pltpu.roll(rows[ext - 8 : ext], 1, 0), rows[2 * height : ext - 8]]
+        below = jnp.concatenate(below, axis=0)
+        odd = lax.rem(me_ref[0], 2) == 1
+        rows = jnp.concatenate(
+            [
+                jnp.where(odd, below, above),
+                rows[height : 2 * height],
+                jnp.where(odd, above, below),
+                jnp.zeros((PC - ext, PC), F32),
+            ],
+            axis=0,
+        ).T[: bases * height]
         high = rows.astype(BF16).astype(F32)
         low = rows - high
         blank = jnp.zeros_like(rows)
@@ -164,7 +183,7 @@
 
 
 def match_kernel(
-    bases, first, last, order, place_ref, fore_ref, back_ref, image_ref, inv_ref, rows_ref, cols_ref,
+    bases, first, last, order, place_ref, far_ref, near_ref, image_ref, inv_ref, rows_ref, cols_ref,
     edge_ref, *refs
 ):
     if first:
@@ -185,30 +204,21 @@
     body = width - tail
     split_at = body // PC
 
-    def unpacked(ref, n, base, spare):
+    def halo(ref, n):
         if n < split_at:
-            return ref[step, :, base + n * PC : base + (n + 1) * PC]
-        parts = []
-        for r in range(8):
-            j = r - (r > spare)
-            at = base + j * tail + (n - split_at) * PC
-            if r == spare:
-                parts.append(jnp.zeros((1, PC), F32))
-            else:
-                parts.append(ref[step, spare : spare + 1, at : at + PC])
-        return jnp.concatenate(parts, axis=0)
+            parts = [ref[step, :, n * PC : (n + 1) * PC]]
+        else:
+            parts = [jnp.zeros((1, PC), F32)]
+            for r in range(1, 8):
+                at = (r - 1) * tail + (n - split_at) * PC
+                parts.append(ref[step, 0:1, at : at + PC])
+        for t in range(height // 8 - 1):
+            at = body + t * width + n * PC
+            parts.append(ref[step, :, at : at + PC])
+        return parts
 
     def column(n):
-        full = height // 8 - 1
-        parts = [unpacked(fore_ref, n, 0, 0)]
-        for t in range(full):
-            at = body + t * width + n * PC
-            parts.append(fore_ref[step, :, at : at + PC])
-        parts.append(image_ref[visit, :, n * PC : (n + 1) * PC])
-        for t in range(full):
-            at = t * width + n * PC
-            parts.append(back_ref[step, :, at : at + PC])
-        parts.append(unpacked(back_ref, n, full * width, 7))
+        parts = halo(far_ref, n) + [image_ref[visit, :, n * PC : (n + 1) * PC]] + halo(near_ref, n)
         if pad > 3 * height:
             parts.append(jnp.zeros((pad - 3 * height, PC), F32))
         return jnp.concatenate(parts, axis=0)
@@ -306,8 +316,8 @@
     for bit in reversed(bits):
         order = order + [slot ^ bit for slot in order]
     order = tuple(order)
-    rising = [(i, i + 1) for i in range(size - 1)]
-    falling = [(j, i) for i, j in rising]
+    near_pairs = [(i, i ^ 1) for i in range(size)]
+    far_pairs = [(i, j) for j in range(size) for i in (j - 1 + 2 * (j % 2),) if 0 <= i < size]
     smem = pl.BlockSpec(memory_space=pltpu.SMEM)
     vmem = pl.BlockSpec(memory_space=pltpu.VMEM)
     anywhere = pl.BlockSpec(memory_space=pl.ANY)
@@ -318,17 +328,17 @@
     halos = []
     for (first, count) in chunks:
         block = pl.BlockSpec((1, 8, lanes), lambda v: (v, 0, 0))
-        fore, back = pl.pallas_call(
+        far, near = pl.pallas_call(
             pack_kernel,
             grid=(count,),
-            in_specs=[pl.BlockSpec((1, height, width), lambda v, first=first: (v + first, 0, 0))],
+            in_specs=[smem, pl.BlockSpec((1, height, width), lambda v, first=first: (v + first, 0, 0))],
             out_specs=[block] * 2,
             out_shape=[jax.ShapeDtypeStruct((count, 8, lanes), F32)] * 2,
-            compiler_params=pltpu.CompilerParams(vmem_limit_bytes=60 * 1024 * 1024),
-        )(image)
-        fore = lax.ppermute(fore, "tile", rising)
-        back = lax.ppermute(back, "tile", falling)
-        halos.append((fore, back))
+            compiler_params=params,
+        )(me, image)
+        far = lax.ppermute(far, "tile", far_pairs)
+        near = lax.ppermute(near, "tile", near_pairs)
+        halos.append((far, near))
 
     half = jax.ShapeDtypeStruct((size // 2, height, PC), F32)
     sums = pltpu.VMEM((2, size, height, PC), F32)
@@ -362,7 +372,7 @@
     )
 
     carried = ()
-    for (first, count), (fore, back) in zip(chunks, halos):
+    for (first, count), (far, near) in zip(chunks, halos):
         last = first + count == visits
         shapes = [jax.ShapeDtypeStruct((visits, height, width), BF16)]
         specs = [pl.BlockSpec((1, height, width), lambda v, first=first: (v + first, 0, 0))]
@@ -397,7 +407,7 @@
                 transcendentals=0,
             ),
         )
-        carried = match(place, fore, back, image, inv_var, *operators, *extra)
+        carried = match(place, far, near, image, inv_var, *operators, *extra)
     matched, keep, send = carried
     received = exchange(send, size, bits[0])
     keep = jnp.concatenate([keep[:, :height] + received, keep[:, height:]], axis=1)

time: 63.4 us -> 62.5 us (0.986)
  Pallas kernels: 23 us -> 15.5 us
  starting transfers between devices: 31 us -> 36.8 us
  local copies, waits for them, and re-layouts: 0.03 us -> 1.45 us
    ppermute x6, starting transfers between devices: 16 us -> 29.5 us  [the longest x3 27.4 us: on_device(): near = lax.ppermute(near, 'tile', near_pairs)]
    ppermute x6, starting transfers between devices: 15 us -> 7.36 us  [exchange(): return lax.ppermute(send, 'tile', [(i, i ^ bit) for i in range(size)])]
    pallas_call x6, Pallas kernels: 17.2 us -> 9.68 us  [the longest x3 9.36 us: on_device(): carried = match(place, far, near, image, inv_var, *operators, *extra)]
    unnamed x14 -> x16, local copies, waits for them, and re-layouts: 0.03 us -> 1.45 us
  transfers between devices with their start and end apart: 12 -> 12, of which waited for: 4 -> 4; matrix products, arithmetic and copies ran while one was open for 0% -> 0% of each run, Pallas kernels for 28% -> 20%
where the time goes in v4:
time: 62.5 us; the launch traced here: 62.3 us
  starting transfers between devices  36.8 us (59%)
  Pallas kernels  15.5 us (25%)
  waiting for transfers between devices  7.03 us (11%)
  local copies, waits for them, and re-layouts  1.45 us (2%)
  between operations  0.85 us (1%)
  other arithmetic  0.66 us (1%)
    ppermute x3, starting transfers between devices, on_device(): near = lax.ppermute(near, 'tile', near_pairs)  27.4 us
    pallas_call x3, Pallas kernels, on_device(): carried = match(place, far, near, image, inv_var, *operators, *extra)  9.36 us
    ppermute x6, starting transfers between devices, exchange(): return lax.ppermute(send, 'tile', [(i, i ^ bit) for i in range(size)])  7.36 us
    ppermute x6, waiting for transfers between devices, exchange(): return lax.ppermute(send, 'tile', [(i, i ^ bit) for i in range(size)])  7.01 us
    pallas_call x1, Pallas kernels, on_device(): prepare(me, shift.T, col_offset, psf_rows.transpose(1, 0, 2), psf_cols.tr...  4.76 us
    ppermute x3, starting transfers between devices, on_device(): far = lax.ppermute(far, 'tile', far_pairs)  2.08 us
    unnamed x16, local copies, waits for them, and re-layouts  1.45 us
  transfers between devices with their start and end apart: 12, of which 4 were waited for; matrix products, arithmetic and copies ran while one was open for 0% of the time, Pallas kernels for 20%

profile of v4, /device:TPU:0, one launch (start us, length us, event | category | flops | bytes accessed | tf_op | source)
XLA Modules:
  0.0 62.3 jit_solution(17633228669096541827)
XLA Ops:
  0.6 0.0 copy-start
  0.6 1.4 %copy-done = f32[4,24,4096]{2,1,0:T(8,128)S(1)} copy-done((f32[4,24,4096]{2,1,0:T(8,128)S(1)}, f32[4,24,4096]{2,1,0:T(8,128)}, u32[]{:S(2)}) %copy-start) | copy-done | bytes 1572888
  2.0 0.2 shard_map.88
  2.2 0.7 %collective-permute-start.4 = (f32[2,8,11776]{2,1,0:T(8,128)S(1)}, f32[2,8,11776]{2,1,0:T(8,128)S(1)}, u32[]{:S(2)}, u32[]{:S(2)}) collective-permute-start(f32[2,8,11776]{2,1,0:T(8,128)S(1)} %get-tuple-element.27), channel_id=1, source_target_pairs={{2,1},{1,2},{4,3},{3,4},{6,5},{5,6},{8,7},{7,8},{10,9},{9,10},{12,... | collective-permute-start | bytes 2261000 | tf_op jit(solution)/shard_map/ppermute | solution.py:339
  2.9 0.0 copy-start.7
  3.0 0.0 copy-start.2
  3.0 4.4 %collective-permute-start.5 = (f32[2,8,11776]{2,1,0:T(8,128)S(1)}, f32[2,8,11776]{2,1,0:T(8,128)S(1)}, u32[]{:S(2)}, u32[]{:S(2)}) collective-permute-start(f32[2,8,11776]{2,1,0:T(8,128)S(1)} %get-tuple-element.28), channel_id=1, source_target_pairs={{0,1},{1,0},{2,3},{3,2},{4,5},{5,4},{6,7},{7,6},{8,9},{9,8},{10,11... | collective-permute-start | bytes 2261000 | tf_op jit(solution)/shard_map/ppermute | solution.py:340
  7.3 0.1 shard_map.87
  7.4 0.7 %collective-permute-start.2 = (f32[1,8,11776]{2,1,0:T(8,128)S(1)}, f32[1,8,11776]{2,1,0:T(8,128)S(1)}, u32[]{:S(2)}, u32[]{:S(2)}) collective-permute-start(f32[1,8,11776]{2,1,0:T(8,128)S(1)} %get-tuple-element.25), channel_id=1, source_target_pairs={{2,1},{1,2},{4,3},{3,4},{6,5},{5,6},{8,7},{7,8},{10,9},{9,10},{12,... | collective-permute-start | bytes 1130504 | tf_op jit(solution)/shard_map/ppermute | solution.py:339
  8.1 0.0 copy-start.3
  8.1 0.0 copy-start.4
  8.1 0.0 copy-start.5
  8.1 0.0 copy-start.6
  8.2 0.0 copy-start.1
  8.2 2.9 %collective-permute-start.3 = (f32[1,8,11776]{2,1,0:T(8,128)S(1)}, f32[1,8,11776]{2,1,0:T(8,128)S(1)}, u32[]{:S(2)}, u32[]{:S(2)}) collective-permute-start(f32[1,8,11776]{2,1,0:T(8,128)S(1)} %get-tuple-element.26), channel_id=1, source_target_pairs={{0,1},{1,0},{2,3},{3,2},{4,5},{5,4},{6,7},{7,6},{8,9},{9,8},{10,11... | collective-permute-start | bytes 1130504 | tf_op jit(solution)/shard_map/ppermute | solution.py:340
  11.1 0.1 shard_map.86
  11.2 0.7 %collective-permute-start = (f32[1,8,11776]{2,1,0:T(8,128)S(1)}, f32[1,8,11776]{2,1,0:T(8,128)S(1)}, u32[]{:S(2)}, u32[]{:S(2)}) collective-permute-start(f32[1,8,11776]{2,1,0:T(8,128)S(1)} %get-tuple-element.20), channel_id=1, source_target_pairs={{2,1},{1,2},{4,3},{3,4},{6,5},{5,6},{8,7},{7,8},{10,9},{9,10},{12,... | collective-permute-start | bytes 1130504 | tf_op jit(solution)/shard_map/ppermute | solution.py:339
  11.9 0.0 collective-permute-done.4.far_ref
  11.9 20.1 %collective-permute-start.1 = (f32[1,8,11776]{2,1,0:T(8,128)S(1)}, f32[1,8,11776]{2,1,0:T(8,128)S(1)}, u32[]{:S(2)}, u32[]{:S(2)}) collective-permute-start(f32[1,8,11776]{2,1,0:T(8,128)S(1)} %get-tuple-element.21), channel_id=1, source_target_pairs={{0,1},{1,0},{2,3},{3,2},{4,5},{5,4},{6,7},{7,6},{8,9},{9,8},{10,11... | collective-permute-start | bytes 1130504 | tf_op jit(solution)/shard_map/ppermute | solution.py:340
  32.0 0.0 copy-done.7
  32.0 0.0 copy-done.2
  32.0 1.1 %weights.1 = (f32[8,24,128]{2,1,0:T(8,128)S(1)}, f32[8,24,128]{2,1,0:T(8,128)S(1)}) custom-call(s32[128]{0:T(128)S(1)} %xor_bitcast_fusion.place_ref, f32[4,24,4096]{2,1,0:T(8,128)S(1)} %copy-done.2), custom_call_target="tpu_custom_call" | custom-call | tf_op jit(solution)/shard_map/weights/pallas_call | solution.py:354
  33.0 0.0 copy-done.3
  33.0 0.0 copy-done.4
  33.1 0.0 copy-done.5
  33.1 0.0 copy-done.6
  33.1 4.8 %prepare.1 = (bf16[4,72,256]{2,1,0:T(8,128)(2,1)S(1)}, bf16[4,768,256]{2,1,0:T(8,128)(2,1)S(1)}, bf16[4,768,256]{2,1,0:T(8,128)(2,1)S(1)}) custom-call(s32[1]{0:T(128)} %bitcast.1.me_ref, f32[2,4]{1,0:T(2,128)S(1)} %bitcast.8, s32[4]{0:T(128)S(1)} %copy-done.6, f32[3,4,41]{2,1,0:T(4,128)S(1)} %bitcast.6, f32[3,4,41]{2,1,0:T(4,128)S(1)} %bitcast.7), custom_call_target="tpu_custom_call" | custom-call | tf_op jit(solution)/shard_map/prepare/pallas_call | solution.py:370
  37.8 0.0 collective-permute-done.5.near_ref
  37.9 0.1 collective-permute-start.6
  37.9 4.1 %shard_map.89 = (bf16[4,24,4096]{2,1,0:T(8,128)(2,1)}, f32[2,16,24,128]{3,2,1,0:T(8,128)S(1)}) custom-call(s32[128]{0:T(128)S(1)} %xor_bitcast_fusion.place_ref, f32[2,8,11776]{2,1,0:T(8,128)S(1)} %collective-permute-done.4.far_ref, f32[2,8,11776]{2,1,0:T(8,128)S(1)} %collective-permute-done.5.near_ref, f32[4,24,4096]{2,1,0:T(8,128)S(1)} %copy-done.1, ...), custom_call_target="tpu_custom_call" | custom-call | flops 905969664 | bytes 3932160 | tf_op jit(solution)/shard_map/pallas_call | solution.py:410
  42.1 0.0 collective-permute-done.2.far_ref
  42.1 0.0 collective-permute-done.3.near_ref
  42.1 2.6 %shard_map.90 = (bf16[4,24,4096]{2,1,0:T(8,128)(2,1)}, f32[2,16,24,128]{3,2,1,0:T(8,128)S(1)}) custom-call(s32[128]{0:T(128)S(1)} %xor_bitcast_fusion.place_ref, f32[1,8,11776]{2,1,0:T(8,128)S(1)} %collective-permute-done.2.far_ref, f32[1,8,11776]{2,1,0:T(8,128)S(1)} %collective-permute-done.3.near_ref, ...), custom_call_target="tpu_custom_call", output_to_operand_aliasing={{0}: (9, {})} | custom-call | flops 452984832 | bytes 1966080 | tf_op jit(solution)/shard_map/pallas_call | solution.py:410
  44.7 0.0 collective-permute-done.6.refs_3_
  44.7 0.0 collective-permute-done.far_ref
  44.7 0.0 collective-permute-done.1.near_ref
  44.7 2.6 %shard_map.91 = (bf16[4,24,4096]{2,1,0:T(8,128)(2,1)}, f32[8,48,128]{2,1,0:T(8,128)S(1)}, f32[8,24,128]{2,1,0:T(8,128)S(1)}) custom-call(s32[128]{0:T(128)S(1)} %xor_bitcast_fusion.place_ref, f32[1,8,11776]{2,1,0:T(8,128)S(1)} %collective-permute-done.far_ref, f32[1,8,11776]{2,1,0:T(8,128)S(1)} %collective-permute-done.1.near_ref, ...), custom_call_target="tpu_custom_call", output_to_operand_aliasing={{0}: (9, {})} | custom-call | flops 452984832 | bytes 1966080 | tf_op jit(solution)/shard_map/pallas_call | solution.py:410
  47.3 0.5 collective-permute-start.7
  47.8 0.9 %collective-permute-done.7 = f32[8,24,128]{2,1,0:T(8,128)S(1)} collective-permute-done((f32[8,24,128]{2,1,0:T(8,128)S(1)}, f32[8,24,128]{2,1,0:T(8,128)S(1)}, u32[]{:S(2)}, u32[]{:S(2)}) %collective-permute-start.7) | collective-permute-done | bytes 98336 | tf_op jit(solution)/shard_map/ppermute | solution.py:301
  48.8 2.8 %collective-permute-start.10 = (f32[2,48,128]{2,1,0:T(8,128)S(1)}, f32[2,48,128]{2,1,0:T(8,128)S(1)}, u32[]{:S(2)}, u32[]{:S(2)}) collective-permute-start(f32[2,48,128]{2,1,0:T(8,128)S(1)} %get-tuple-element.39), channel_id=1, source_target_pairs={{0,2},{1,3},{2,0},{3,1},{4,6},{5,7},{6,4},{7,5},{8,10},{9,11},{10,... | collective-permute-start | bytes 147464 | tf_op jit(solution)/shard_map/ppermute | solution.py:301
  51.5 1.1 %collective-permute-start.8 = (f32[2,48,128]{2,1,0:T(8,128)S(1)}, f32[2,48,128]{2,1,0:T(8,128)S(1)}, u32[]{:S(2)}, u32[]{:S(2)}) collective-permute-start(f32[2,48,128]{2,1,0:T(8,128)S(1)} %get-tuple-element.38), channel_id=1, source_target_pairs={{0,6},{1,7},{2,4},{3,5},{4,2},{5,3},{6,0},{7,1},{8,14},{9,15},{10,... | collective-permute-start | bytes 147464 | tf_op jit(solution)/shard_map/ppermute | solution.py:301
  52.6 0.5 collective-permute-start.9
  53.1 0.6 collective-permute-done.10
  53.7 3.2 %collective-permute-done.8 = f32[2,48,128]{2,1,0:T(8,128)S(1)} collective-permute-done((f32[2,48,128]{2,1,0:T(8,128)S(1)}, f32[2,48,128]{2,1,0:T(8,128)S(1)}, u32[]{:S(2)}, u32[]{:S(2)}) %collective-permute-start.8) | collective-permute-done | bytes 49184 | tf_op jit(solution)/shard_map/ppermute | solution.py:301
  56.9 0.0 collective-permute-done.9
  56.9 2.5 %collective-permute-start.11 = (f32[1,48,128]{2,1,0:T(8,128)S(1)}, f32[1,48,128]{2,1,0:T(8,128)S(1)}, u32[]{:S(2)}, u32[]{:S(2)}) collective-permute-start(f32[1,48,128]{2,1,0:T(8,128)S(1)} %slice.47), channel_id=1, source_target_pairs={{0,8},{1,9},{2,10},{3,11},{4,12},{5,13},{6,14},{7,15},{8,0},{9,1},... | collective-permute-start | bytes 73736 | tf_op jit(solution)/shard_map/ppermute | solution.py:301
  59.4 2.3 %collective-permute-done.11 = f32[1,48,128]{2,1,0:T(8,128)S(1)} collective-permute-done((f32[1,48,128]{2,1,0:T(8,128)S(1)}, f32[1,48,128]{2,1,0:T(8,128)S(1)}, u32[]{:S(2)}, u32[]{:S(2)}) %collective-permute-start.11) | collective-permute-done | bytes 24608 | tf_op jit(solution)/shard_map/ppermute | solution.py:301
  61.7 0.6 fusion.6
  (7 shorter events, 0.1 us)
Async XLA Ops:
  0.6 1.4 %copy-start = (f32[4,24,4096]{2,1,0:T(8,128)S(1)}, f32[4,24,4096]{2,1,0:T(8,128)}, u32[]{:S(2)}) copy-start(f32[4,24,4096]{2,1,0:T(8,128)} %image_ref.11) | copy-start | bytes 4718596
  2.2 9.6 %collective-permute-start.4 = (f32[2,8,11776]{2,1,0:T(8,128)S(1)}, f32[2,8,11776]{2,1,0:T(8,128)S(1)}, u32[]{:S(2)}, u32[]{:S(2)}) collective-permute-start(f32[2,8,11776]{2,1,0:T(8,128)S(1)} %get-tuple-element.27), channel_id=1, source_target_pairs={{2,1},{1,2},{4,3},{3,4},{6,5},{5,6},{8,7},{7,8},{10,9},{9,10},{12,... | collective-permute-start | bytes 2261000 | tf_op jit(solution)/shard_map/ppermute | solution.py:339
  2.9 29.0 %copy-start.7 = (s32[128,1]{0,1:T(1,128)S(1)}, s32[128,1]{0,1:T(1,128)}, u32[]{:S(2)}) copy-start(s32[128,1]{0,1:T(1,128)} %param.13) | copy-start | bytes 1540
  3.0 29.0 %copy-start.2 = (f32[4,24,4096]{2,1,0:T(8,128)S(1)}, f32[4,24,4096]{2,1,0:T(8,128)}, u32[]{:S(2)}) copy-start(f32[4,24,4096]{2,1,0:T(8,128)} %inv_ref.7) | copy-start | bytes 4718596
  3.0 34.9 %collective-permute-start.5 = (f32[2,8,11776]{2,1,0:T(8,128)S(1)}, f32[2,8,11776]{2,1,0:T(8,128)S(1)}, u32[]{:S(2)}, u32[]{:S(2)}) collective-permute-start(f32[2,8,11776]{2,1,0:T(8,128)S(1)} %get-tuple-element.28), channel_id=1, source_target_pairs={{0,1},{1,0},{2,3},{3,2},{4,5},{5,4},{6,7},{7,6},{8,9},{9,8},{10,11... | collective-permute-start | bytes 2261000 | tf_op jit(solution)/shard_map/ppermute | solution.py:340
  7.4 34.6 %collective-permute-start.2 = (f32[1,8,11776]{2,1,0:T(8,128)S(1)}, f32[1,8,11776]{2,1,0:T(8,128)S(1)}, u32[]{:S(2)}, u32[]{:S(2)}) collective-permute-start(f32[1,8,11776]{2,1,0:T(8,128)S(1)} %get-tuple-element.25), channel_id=1, source_target_pairs={{2,1},{1,2},{4,3},{3,4},{6,5},{5,6},{8,7},{7,8},{10,9},{9,10},{12,... | collective-permute-start | bytes 1130504 | tf_op jit(solution)/shard_map/ppermute | solution.py:339
  8.1 24.9 %copy-start.3 = (f32[4,3,41]{2,0,1:T(4,128)S(1)}, f32[4,3,41]{2,0,1:T(4,128)}, u32[]{:S(2)}) copy-start(f32[4,3,41]{2,0,1:T(4,128)} %param.11) | copy-start | bytes 5908
  8.1 24.9 %copy-start.4 = (f32[4,3,41]{2,0,1:T(4,128)S(1)}, f32[4,3,41]{2,0,1:T(4,128)}, u32[]{:S(2)}) copy-start(f32[4,3,41]{2,0,1:T(4,128)} %param.12) | copy-start | bytes 5908
  8.1 24.9 %copy-start.5 = (f32[4,2]{0,1:T(2,128)S(1)}, f32[4,2]{0,1:T(2,128)}, u32[]{:S(2)}) copy-start(f32[4,2]{0,1:T(2,128)} %param.9) | copy-start | bytes 100
  8.1 24.9 %copy-start.6 = (s32[4]{0:T(128)S(1)}, s32[4]{0:T(128)}, u32[]{:S(2)}) copy-start(s32[4]{0:T(128)} %offset_ref.1) | copy-start | bytes 52
  8.2 29.8 %copy-start.1 = (f32[4,24,4096]{2,1,0:T(8,128)S(1)}, f32[4,24,4096]{2,1,0:T(8,128)}, u32[]{:S(2)}) copy-start(f32[4,24,4096]{2,1,0:T(8,128)} %image_ref.11) | copy-start | bytes 4718596
  8.2 33.9 %collective-permute-start.3 = (f32[1,8,11776]{2,1,0:T(8,128)S(1)}, f32[1,8,11776]{2,1,0:T(8,128)S(1)}, u32[]{:S(2)}, u32[]{:S(2)}) collective-permute-start(f32[1,8,11776]{2,1,0:T(8,128)S(1)} %get-tuple-element.26), channel_id=1, source_target_pairs={{0,1},{1,0},{2,3},{3,2},{4,5},{5,4},{6,7},{7,6},{8,9},{9,8},{10,11... | collective-permute-start | bytes 1130504 | tf_op jit(solution)/shard_map/ppermute | solution.py:340
  11.2 33.5 %collective-permute-start = (f32[1,8,11776]{2,1,0:T(8,128)S(1)}, f32[1,8,11776]{2,1,0:T(8,128)S(1)}, u32[]{:S(2)}, u32[]{:S(2)}) collective-permute-start(f32[1,8,11776]{2,1,0:T(8,128)S(1)} %get-tuple-element.20), channel_id=1, source_target_pairs={{2,1},{1,2},{4,3},{3,4},{6,5},{5,6},{8,7},{7,8},{10,9},{9,10},{12,... | collective-permute-start | bytes 1130504 | tf_op jit(solution)/shard_map/ppermute | solution.py:339
  11.9 32.8 %collective-permute-start.1 = (f32[1,8,11776]{2,1,0:T(8,128)S(1)}, f32[1,8,11776]{2,1,0:T(8,128)S(1)}, u32[]{:S(2)}, u32[]{:S(2)}) collective-permute-start(f32[1,8,11776]{2,1,0:T(8,128)S(1)} %get-tuple-element.21), channel_id=1, source_target_pairs={{0,1},{1,0},{2,3},{3,2},{4,5},{5,4},{6,7},{7,6},{8,9},{9,8},{10,11... | collective-permute-start | bytes 1130504 | tf_op jit(solution)/shard_map/ppermute | solution.py:340
  37.9 6.8 %collective-permute-start.6 = (f32[8,24,128]{2,1,0:T(8,128)S(1)}, f32[8,24,128]{2,1,0:T(8,128)S(1)}, u32[]{:S(2)}, u32[]{:S(2)}) collective-permute-start(f32[8,24,128]{2,1,0:T(8,128)S(1)} %get-tuple-element.34), channel_id=1, source_target_pairs={{0,1},{1,0},{2,3},{3,2},{4,5},{5,4},{6,7},{7,6},{8,9},{9,8},{10,11... | collective-permute-start | bytes 294920 | tf_op jit(solution)/shard_map/ppermute | solution.py:301
  47.3 1.4 %collective-permute-start.7 = (f32[8,24,128]{2,1,0:T(8,128)S(1)}, f32[8,24,128]{2,1,0:T(8,128)S(1)}, u32[]{:S(2)}, u32[]{:S(2)}) collective-permute-start(f32[8,24,128]{2,1,0:T(8,128)S(1)} %get-tuple-element.37), channel_id=1, source_target_pairs={{0,1},{1,0},{2,3},{3,2},{4,5},{5,4},{6,7},{7,6},{8,9},{9,8},{10,11... | collective-permute-start | bytes 294920 | tf_op jit(solution)/shard_map/ppermute | solution.py:301
  48.8 5.0 %collective-permute-start.10 = (f32[2,48,128]{2,1,0:T(8,128)S(1)}, f32[2,48,128]{2,1,0:T(8,128)S(1)}, u32[]{:S(2)}, u32[]{:S(2)}) collective-permute-start(f32[2,48,128]{2,1,0:T(8,128)S(1)} %get-tuple-element.39), channel_id=1, source_target_pairs={{0,2},{1,3},{2,0},{3,1},{4,6},{5,7},{6,4},{7,5},{8,10},{9,11},{10,... | collective-permute-start | bytes 147464 | tf_op jit(solution)/shard_map/ppermute | solution.py:301
  51.5 5.3 %collective-permute-start.8 = (f32[2,48,128]{2,1,0:T(8,128)S(1)}, f32[2,48,128]{2,1,0:T(8,128)S(1)}, u32[]{:S(2)}, u32[]{:S(2)}) collective-permute-start(f32[2,48,128]{2,1,0:T(8,128)S(1)} %get-tuple-element.38), channel_id=1, source_target_pairs={{0,6},{1,7},{2,4},{3,5},{4,2},{5,3},{6,0},{7,1},{8,14},{9,15},{10,... | collective-permute-start | bytes 147464 | tf_op jit(solution)/shard_map/ppermute | solution.py:301
  52.6 4.2 %collective-permute-start.9 = (f32[2,48,128]{2,1,0:T(8,128)S(1)}, f32[2,48,128]{2,1,0:T(8,128)S(1)}, u32[]{:S(2)}, u32[]{:S(2)}) collective-permute-start(f32[2,48,128]{2,1,0:T(8,128)S(1)} %get-tuple-element.40), channel_id=1, source_target_pairs={{0,4},{1,5},{2,6},{3,7},{4,0},{5,1},{6,2},{7,3},{8,12},{9,13},{10,... | collective-permute-start | bytes 147464 | tf_op jit(solution)/shard_map/ppermute | solution.py:301
  56.9 4.8 %collective-permute-start.11 = (f32[1,48,128]{2,1,0:T(8,128)S(1)}, f32[1,48,128]{2,1,0:T(8,128)S(1)}, u32[]{:S(2)}, u32[]{:S(2)}) collective-permute-start(f32[1,48,128]{2,1,0:T(8,128)S(1)} %slice.47), channel_id=1, source_target_pairs={{0,8},{1,9},{2,10},{3,11},{4,12},{5,13},{6,14},{7,15},{8,0},{9,1},... | collective-permute-start | bytes 73736 | tf_op jit(solution)/shard_map/ppermute | solution.py:301
